TPU v7x, 128 devices: a whole 4x4x4 slice. The times are simulated.
128 devices in a mesh: row: 16 (over x, z), col: 8 (over y, core).
Axes of the slice: x: 4, y: 4, z: 4, core: 2. Of those that a mesh axis runs over, the one named last changes fastest.
Arguments:
- primal_rows: bfloat16 [16384, 8192], P('row', 'col'), may hold values from -6 to 6
- dual_rows: bfloat16 [16384, 8192], P('row', 'col'), may hold values from -6 to 6
- weight_rows: bfloat16 [16384, 8192], P('row', 'col'), may hold values from -0.0625 to 0.0625
- pairs: int32 [384, 2], P('row'), may hold values from 0 to 63, as said below
Outputs:
- tiles: float32 [384, 256, 256], P('row', 'col')
Inputs may be any that keep to these rules, and one draw needn't show every extreme that they name: `pairs`: tile rows r * 24 to (r + 1) * 24 - 1 have their first block i among blocks r * 4 to (r + 1) * 4 - 1. Among their second blocks j, the blocks held by any other row index q (blocks q * 4 to (q + 1) * 4 - 1) are exactly one block, named one or more times; blocks of r itself may appear too.
All inputs are finite; a program needn't handle non-finite values.
Results may differ from a plain program's by a relative error of at most 0.0003.
Values may be sent and summed in bfloat16 or wider, within the bound.
No kernel may reach another device: no remote copies, remote signals or barrier semaphores. Data moves between devices by JAX's collectives and lax.ppermute only.
A program may use at most 128 MiB of HBM per device.

v0:
```python
import functools

import jax
import jax.numpy as jnp
from jax import lax
from jax.experimental import pallas as pl
from jax.experimental.pallas import tpu as pltpu
from jax.sharding import PartitionSpec as P


TILE = 256
SIDE = 4
WIDTHS = (64, 64)
LANES = 128
ROWS = 32
TOP = 32700.0
LENGTH = 16 * ROWS + 16

ANY = pl.BlockSpec(memory_space=pl.ANY)
SMEM = pl.BlockSpec(memory_space=pltpu.SMEM)
VMEM = pl.BlockSpec(memory_space=pltpu.VMEM)


def shift_x(value, step):
    perm = [(r, ((r // SIDE + step) % SIDE) * SIDE + r % SIDE) for r in range(SIDE * SIDE)]
    return lax.ppermute(value, "row", perm)


def shift_z(value, step):
    perm = [(r, (r // SIDE) * SIDE + (r % SIDE + step) % SIDE) for r in range(SIDE * SIDE)]
    return lax.ppermute(value, "row", perm)


def shift_y(value, step):
    perm = [(c, ((c // 2 + step) % SIDE) * 2 + c % 2) for c in range(SIDE * 2)]
    return lax.ppermute(value, "col", perm)


def swap_cores(value):
    return lax.ppermute(value, "col", [(c, c ^ 1) for c in range(SIDE * 2)])


def pick_kernel(offset, *refs):
    wants_z, wants_x = refs[0:4], refs[4:8]
    held = (refs[8:13], refs[13:18])
    outs = (refs[18:22], refs[22:26])
    sems = refs[26]
    part = pl.ds(offset, outs[0][0].shape[1])
    row = lax.axis_index("row")
    x, z = row // SIDE, row % SIDE
    waits = []
    for half in range(2):
        own, plus, minus, far_low, far_high = held[half]
        for away in range(SIDE):
            for near in range(SIDE):
                if away == 0 and near == 0:
                    continue
                if half == 0:
                    choice = wants_z[away][((x + SIDE - near) % SIDE) * SIDE + z]
                else:
                    choice = wants_x[away][x * SIDE + (z + SIDE - near) % SIDE]
                target = outs[half][away].at[near]
                sem = sems.at[half, away, near]
                if near == 2:
                    @pl.when(choice < 2)
                    def _():
                        pltpu.make_async_copy(far_low.at[choice, part], target, sem).start()

                    @pl.when(choice >= 2)
                    def _():
                        pltpu.make_async_copy(far_high.at[choice - 2, part], target, sem).start()
                else:
                    origin = {0: own, 1: plus, 3: minus}[near]
                    pltpu.make_async_copy(origin.at[choice, part], target, sem).start()
                waits.append(pltpu.make_async_copy(own.at[0, part], target, sem))
    for copy in waits:
        copy.wait()


def pick(wants_z, wants_x, held_a, held_b, offset, rows):
    piece = jax.ShapeDtypeStruct((SIDE, rows, held_a[0].shape[2]), held_a[0].dtype)
    outs = pl.pallas_call(
        functools.partial(pick_kernel, offset),
        out_shape=[piece] * 8,
        in_specs=[SMEM] * 8 + [ANY] * 10,
        out_specs=[VMEM] * 8,
        scratch_shapes=[pltpu.SemaphoreType.DMA((2, SIDE, SIDE))],
    )(*wants_z, *wants_x, *held_a, *held_b)
    return outs[:4], outs[4:]


def encode(value, out):
    count = value.shape[0]
    peak = jnp.maximum(jnp.max(jnp.abs(value), axis=1), 1e-30)
    level = jnp.ceil(jnp.log2(peak) * 256.0)
    factor = jnp.exp2(level * (-1.0 / 256.0)) * TOP
    code = jnp.round(value * factor[:, None, :]).astype(jnp.int32).astype(jnp.int16)
    out[pl.ds(0, count * ROWS)] = code.reshape(count * ROWS, LANES)
    out[pl.ds(count * ROWS, count)] = level.astype(jnp.int32).astype(jnp.int16)


def product_kernel(offset, rows, slots, *refs):
    group_first, group_start, slot_tile, slot_a, slot_b = refs[0:5]
    lefts = refs[5:9]
    tables = (refs[9:14], refs[14:19])
    kept, coded = refs[19], refs[20:23]
    left, held_a, held_b, acc, sems, left_sems, out_sem = refs[23:]
    y = lax.axis_index("col") // 2
    features = lefts[0].shape[2]
    width = 2 * rows
    group = TILE // width
    blocks = kept.shape[0]
    copies = []
    for half, held in enumerate((held_a, held_b)):
        for place in range(5):
            source = tables[half][place]
            if place == 4:
                source = source.at[:, pl.ds(offset, rows)]
            copies.append(
                pltpu.make_async_copy(source, held.at[pl.ds(place * SIDE, SIDE)], sems.at[half, place])
            )
    left_copies = []
    for block in range(SIDE):
        for n in range(4):
            target = left.at[block, pl.ds(n % 2 * TILE, TILE), pl.ds(n // 2 * features, features)]
            left_copies.append(pltpu.make_async_copy(lefts[n].at[block], target, left_sems.at[block, n]))
    for copy in copies + left_copies:
        copy.start()
    for copy in copies:
        copy.wait()

    def one(slot, carry):
        for block in range(SIDE):
            @pl.when(group_start[block] == slot)
            def _():
                for copy in left_copies[4 * block : 4 * block + 4]:
                    copy.wait()

        right = []
        for g in range(group):
            right += [held_a[slot_a[slot * group + g]], held_b[slot_b[slot * group + g]]]
        out = lax.dot_general(
            left[group_first[slot]],
            jnp.concatenate(right, axis=0),
            (((1,), (1,)), ((), ())),
            preferred_element_type=jnp.float32,
        )
        for g in range(group):
            tile = slot_tile[slot * group + g]
            cross_x = out[:TILE, g * width : (g + 1) * width]
            cross_s = out[TILE:, g * width : (g + 1) * width]
            parts = jnp.concatenate([cross_x, cross_s], axis=1).reshape(SIDE, 2, ROWS, LANES)
            for target in range(SIDE):
                away = (target + SIDE - y) % SIDE
                acc[away, pl.ds(tile * 2, 2)] = parts[target]
        return carry

    lax.fori_loop(0, slots, one, 0, unroll=3)
    for block in range(SIDE):
        @pl.when(group_start[block] >= slots)
        def _():
            for copy in left_copies[4 * block : 4 * block + 4]:
                copy.wait()

    keep = pltpu.make_async_copy(acc.at[0, pl.ds(0, blocks)], kept, out_sem)
    keep.start()
    for d in range(1, SIDE):
        for start in range(0, blocks, 16):
            encode(acc[d, pl.ds(start, 16)], coded[d - 1].at[pl.ds(start // 16 * LENGTH, LENGTH)])
    keep.wait()


def grouped(first, spot_a, spot_b, group):
    tiles = first.shape[0]
    slots = (tiles + (group - 1) * SIDE) // group
    kinds = jnp.arange(SIDE, dtype=jnp.int32)
    order = jnp.arange(tiles, dtype=jnp.int32)
    same = first[:, None] == first[None, :]
    rank = jnp.sum(jnp.where(same & (order[None, :] < order[:, None]), 1, 0), axis=1)
    counts = jnp.sum(jnp.where(first[None, :] == kinds[:, None], 1, 0), axis=1)
    sizes = (counts + group - 1) // group
    starts = jnp.sum(jnp.where(kinds[None, :] < kinds[:, None], sizes[None, :], 0), axis=1)
    start = jnp.sum(jnp.where(first[:, None] == kinds[None, :], starts[None, :], 0), axis=1)
    place = start * group + rank
    chosen = place[None, :] == jnp.arange(slots * group, dtype=jnp.int32)[:, None]
    used = jnp.any(chosen, axis=1)
    pull = lambda v: jnp.sum(jnp.where(chosen, v[None, :], 0), axis=1)
    slot_tile = jnp.where(used, pull(order), tiles)
    slot_a = jnp.where(used, pull(spot_a), 16)
    slot_b = jnp.where(used, pull(spot_b), 16)
    past = jnp.arange(slots, dtype=jnp.int32)[:, None] >= starts[None, :]
    group_first = jnp.sum(jnp.where(past, 1, 0), axis=1) - 1
    return slots, (group_first, starts, slot_tile, slot_a, slot_b)


def products(lists, slots, lefts, table_a, table_b, offset, rows, tiles):
    features = 2 * lefts[0].shape[2]
    blocks = 2 * tiles
    code = jax.ShapeDtypeStruct((blocks // 16 * LENGTH, LANES), jnp.int16)
    return pl.pallas_call(
        functools.partial(product_kernel, offset, rows, slots),
        out_shape=[jax.ShapeDtypeStruct((blocks, ROWS, LANES), jnp.float32)] + [code] * 3,
        in_specs=[SMEM] * 5 + [ANY] * 14,
        out_specs=[ANY] + [VMEM] * 3,
        scratch_shapes=[
            pltpu.VMEM((SIDE, 2 * TILE, features), jnp.bfloat16),
            pltpu.VMEM((20, rows, features), jnp.bfloat16),
            pltpu.VMEM((20, rows, features), jnp.bfloat16),
            pltpu.VMEM((SIDE, blocks + 2, ROWS, LANES), jnp.float32),
            pltpu.SemaphoreType.DMA((2, 5)),
            pltpu.SemaphoreType.DMA((SIDE, 4)),
            pltpu.SemaphoreType.DMA,
        ],
    )(*lists, *lefts, *table_a, *table_b)


def finish_kernel(kept, *refs):
    coded, mine, theirs = refs[:3], refs[3], refs[4]
    core = lax.axis_index("col") % 2
    count = kept.shape[0]
    total = kept[...]
    for ref in coded:
        code = ref[pl.ds(0, count * ROWS)].astype(jnp.int32).astype(jnp.float32)
        level = ref[pl.ds(count * ROWS, count)].astype(jnp.int32).astype(jnp.float32)
        factor = jnp.exp2(level * (1.0 / 256.0)) * (1.0 / TOP)
        total = total + code.reshape(count, ROWS, LANES) * factor[:, None, :]
    pairs = (total[..., : LANES // 2] * total[..., LANES // 2 :]).reshape(count // 2, 2, ROWS, LANES // 2)
    mine[...] = jnp.where(core == 0, pairs[:, 0], pairs[:, 1])
    theirs[...] = jnp.where(core == 0, pairs[:, 1], pairs[:, 0])


def finish(kept, coded):
    blocks = kept.shape[0]
    steps = blocks // 16
    out_block = pl.BlockSpec((8, ROWS, LANES // 2), lambda s: (s, 0, 0))
    return pl.pallas_call(
        finish_kernel,
        grid=(steps,),
        out_shape=[jax.ShapeDtypeStruct((8 * steps, ROWS, LANES // 2), jnp.float32)] * 2,
        in_specs=[pl.BlockSpec((16, ROWS, LANES), lambda s: (s, 0, 0))]
        + [pl.BlockSpec((LENGTH, LANES), lambda s: (s, 0))] * 3,
        out_specs=[out_block, out_block],
        name="finish",
    )(kept, *coded)


def gather_ring(own, shift):
    plus = shift(own, 1)
    minus = shift(own, SIDE - 1)
    far_low = shift(plus[:2], 1)
    far_high = shift(minus[2:], SIDE - 1)
    return own, plus, minus, far_low, far_high


def shards(primal_rows, dual_rows, weight_rows, pairs):
    row = lax.axis_index("row")
    x, z = row // SIDE, row % SIDE
    features = primal_rows.shape[1]
    blocks = primal_rows.shape[0] // TILE
    tiles = pairs.shape[0]
    core = lax.axis_index("col") % 2
    weight = weight_rows.reshape(blocks, TILE, features)
    columns = TILE // 2
    starts = [sum(WIDTHS[:k]) for k in range(len(WIDTHS))]
    given = lax.dynamic_slice_in_dim(weight, (1 - core) * columns, columns, 1)
    gotten = swap_cores(given)
    owned = lax.dynamic_slice_in_dim(weight, core * columns, columns, 1)
    owned = jnp.concatenate([owned, gotten], axis=2)
    half_a = [owned[:, s : s + w // 2] for s, w in zip(starts, WIDTHS)]
    half_b = [owned[:, s + w // 2 : s + w] for s, w in zip(starts, WIDTHS)]
    held_a = gather_ring(jnp.concatenate(half_a, axis=1), shift_x)
    held_b = gather_ring(jnp.concatenate(half_b, axis=1), shift_z)
    lefts = [primal_rows, dual_rows, swap_cores(primal_rows), swap_cores(dual_rows)]
    lefts = [v.reshape(blocks, TILE, features) for v in lefts]

    second = pairs[:, 1]
    owner, local = second // blocks, second % blocks
    hit = owner[:, None] == jnp.arange(SIDE * SIDE, dtype=jnp.int32)[None, :]
    want = jnp.max(jnp.where(hit, local[:, None], 0), axis=0)
    wants_z = [want] + [shift_z(want, SIDE - d) for d in range(1, SIDE)]
    wants_x = [want] + [shift_x(want, SIDE - d) for d in range(1, SIDE)]
    dx = (x + SIDE - owner // SIDE) % SIDE
    dz = (z + SIDE - owner % SIDE) % SIDE
    spot_a = jnp.where(owner == row, 16 + local, dz * SIDE + dx)
    spot_b = jnp.where(owner == row, 16 + local, dx * SIDE + dz)
    first = pairs[:, 0] % blocks

    arrived = []
    for start, width in zip(starts, WIDTHS):
        send_a, send_b = pick(wants_z, wants_x, held_a, held_b, start // 2, width // 2)
        table_a = [send_a[0]] + [shift_z(send_a[d], d) for d in range(1, SIDE)] + [held_a[0]]
        table_b = [send_b[0]] + [shift_x(send_b[d], d) for d in range(1, SIDE)] + [held_b[0]]
        arrived.append((table_a, table_b))
    outs = []
    for (table_a, table_b), start, width in zip(arrived, starts, WIDTHS):
        slots, lists = grouped(first, spot_a, spot_b, TILE // width)
        kept, *coded = products(
            lists, slots, lefts, table_a, table_b, start // 2, width // 2, tiles
        )
        moved = [shift_y(code, d + 1) for d, code in enumerate(coded)]
        mine, theirs = finish(kept, moved)
        outs.append((mine, swap_cores(theirs)))
    mine = jnp.concatenate([m for m, _ in outs], axis=-1)
    theirs = jnp.concatenate([t for _, t in outs], axis=-1)
    low = jnp.where(core == 0, mine, theirs)
    high = jnp.where(core == 0, theirs, mine)
    return jnp.concatenate([low, high], axis=-1)


def solution(mesh):
    placed = (P("row", "col"), P("row", "col"), P("row", "col"), P("row", None))
    return jax.shard_map(
        shards, mesh=mesh, in_specs=placed, out_specs=P("row", "col", None), check_vma=False
    )
```

profile of v0, /device:TPU:1, one launch (start us, length us, event | category | flops | bytes accessed | tf_op | source)
XLA Modules:
  0.0 191.3 jit_solution(2338341995873077639)
XLA Ops:
  13.8 19.1 %collective-permute-done.13.refs_14_ = bf16[4,64,2048]{2,1,0:T(8,128)(2,1)S(1)} collective-permute-done((bf16[4,64,2048]{2,1,0:T(8,128)(2,1)S(1)}, bf16[4,64,2048]{2,1,0:T(8,128)(2,1)S(1)}, u32[]{:S(2)}, u32[]{:S(2)}) %collective-permute-start.13) | collective-permute-done | bytes 1048608 | tf_op jit(solution)/shard_map/ppermute | solution.py:31
  35.3 2.7 %collective-permute-start.2 = (s32[16]{0:T(128)S(1)}, s32[16]{0:T(128)S(1)}, u32[]{:S(2)}, u32[]{:S(2)}) collective-permute-start(s32[16]{0:T(128)S(1)} %select_reduce_fusion.4.refs_0_.refs_4_), channel_id=1, source_target_pairs={{0,24},{8,0},{16,8},{24,16},{32,56},{40,32},{48,40},{56,48},{64,88... | collective-permute-start | bytes 200 | tf_op jit(solution)/shard_map/ppermute | solution.py:31
  41.1 6.0 %collective-permute-done.3.refs_2_ = s32[16]{0:T(128)S(1)} collective-permute-done((s32[16]{0:T(128)S(1)}, s32[16]{0:T(128)S(1)}, u32[]{:S(2)}, u32[]{:S(2)}) %collective-permute-start.3) | collective-permute-done | bytes 96 | tf_op jit(solution)/shard_map/ppermute | solution.py:31
  47.1 2.5 %collective-permute-start.5 = (s32[16]{0:T(128)S(1)}, s32[16]{0:T(128)S(1)}, u32[]{:S(2)}, u32[]{:S(2)}) collective-permute-start(s32[16]{0:T(128)S(1)} %select_reduce_fusion.4.refs_0_.refs_4_), channel_id=1, source_target_pairs={{0,96},{8,104},{16,112},{24,120},{32,0},{40,8},{48,16},{56,24},{64... | collective-permute-start | bytes 200 | tf_op jit(solution)/shard_map/ppermute | solution.py:26
  55.1 2.7 %collective-permute-start.12 = (bf16[2,64,2048]{2,1,0:T(8,128)(2,1)S(1)}, bf16[2,64,2048]{2,1,0:T(8,128)(2,1)S(1)}, u32[]{:S(2)}, u32[]{:S(2)}) collective-permute-start(bf16[2,64,2048]{2,1,0:T(8,128)(2,1)S(1)} %slice.45), channel_id=1, source_target_pairs={{0,96},{8,104},{16,112},{24,120},{32,0},{40,8},{48,16},{56,24},{64... | collective-permute-start | bytes 1572872 | tf_op jit(solution)/shard_map/ppermute | solution.py:26
  57.9 5.2 %collective-permute-done.16.refs_17_ = bf16[2,64,2048]{2,1,0:T(8,128)(2,1)S(1)} collective-permute-done((bf16[2,64,2048]{2,1,0:T(8,128)(2,1)S(1)}, bf16[2,64,2048]{2,1,0:T(8,128)(2,1)S(1)}, u32[]{:S(2)}, u32[]{:S(2)}) %collective-permute-start.16) | collective-permute-done | bytes 524320 | tf_op jit(solution)/shard_map/ppermute | solution.py:31
  63.2 3.2 %collective-permute-done.11.refs_11_ = bf16[2,64,2048]{2,1,0:T(8,128)(2,1)S(1)} collective-permute-done((bf16[2,64,2048]{2,1,0:T(8,128)(2,1)S(1)}, bf16[2,64,2048]{2,1,0:T(8,128)(2,1)S(1)}, u32[]{:S(2)}, u32[]{:S(2)}) %collective-permute-start.11) | collective-permute-done | bytes 524320 | tf_op jit(solution)/shard_map/ppermute | solution.py:26
  68.0 5.3 %shard_map.46 = (bf16[4,32,2048]{2,1,0:T(8,128)(2,1)}, bf16[4,32,2048]{2,1,0:T(8,128)(2,1)}, bf16[4,32,2048]{2,1,0:T(8,128)(2,1)}, bf16[4,32,2048]{2,1,0:T(8,128...) custom-call(s32[16]{0:T(128)} %copy-done.21, ...), custom_call_target="tpu_custom_call" | custom-call | tf_op jit(solution)/shard_map/pallas_call | solution.py:82
  73.8 2.6 %collective-permute-start.19 = (bf16[4,32,2048]{2,1,0:T(8,128)(2,1)}, bf16[4,32,2048]{2,1,0:T(8,128)(2,1)S(1)}, u32[]{:S(2)}, u32[]{:S(2)}) collective-permute-start(bf16[4,32,2048]{2,1,0:T(8,128)(2,1)} %get-tuple-element.36), channel_id=1, source_target_pairs={{0,24},{8,0},{16,8},{24,16},{32,56},{40,32},{48,40},{56,48},{64,88... | collective-permute-start | bytes 1572872 | tf_op jit(solution)/shard_map/ppermute | solution.py:31
  76.4 5.3 %shard_map.48 = (bf16[4,32,2048]{2,1,0:T(8,128)(2,1)}, bf16[4,32,2048]{2,1,0:T(8,128)(2,1)}, bf16[4,32,2048]{2,1,0:T(8,128)(2,1)}, bf16[4,32,2048]{2,1,0:T(8,128...) custom-call(s32[16]{0:T(128)} %copy-done.21, ...), custom_call_target="tpu_custom_call" | custom-call | tf_op jit(solution)/shard_map/pallas_call | solution.py:82
  81.8 2.8 %collective-permute-start.21 = (bf16[4,32,2048]{2,1,0:T(8,128)(2,1)}, bf16[4,32,2048]{2,1,0:T(8,128)(2,1)S(1)}, u32[]{:S(2)}, u32[]{:S(2)}) collective-permute-start(bf16[4,32,2048]{2,1,0:T(8,128)(2,1)} %get-tuple-element.39), channel_id=1, source_target_pairs={{0,64},{8,72},{16,80},{24,88},{32,96},{40,104},{48,112},{56,120},{... | collective-permute-start | bytes 1572872 | tf_op jit(solution)/shard_map/ppermute | solution.py:26
  84.6 3.3 %collective-permute-done.17.refs_10_ = bf16[4,32,2048]{2,1,0:T(8,128)(2,1)S(1)} collective-permute-done((bf16[4,32,2048]{2,1,0:T(8,128)(2,1)}, bf16[4,32,2048]{2,1,0:T(8,128)(2,1)S(1)}, u32[]{:S(2)}, u32[]{:S(2)}) %collective-permute-start.17) | collective-permute-done | bytes 524320 | tf_op jit(solution)/shard_map/ppermute | solution.py:31
  87.9 4.5 %collective-permute-done.18.refs_11_ = bf16[4,32,2048]{2,1,0:T(8,128)(2,1)S(1)} collective-permute-done((bf16[4,32,2048]{2,1,0:T(8,128)(2,1)}, bf16[4,32,2048]{2,1,0:T(8,128)(2,1)S(1)}, u32[]{:S(2)}, u32[]{:S(2)}) %collective-permute-start.18) | collective-permute-done | bytes 524320 | tf_op jit(solution)/shard_map/ppermute | solution.py:31
  92.5 6.9 %collective-permute-done.19.refs_12_ = bf16[4,32,2048]{2,1,0:T(8,128)(2,1)S(1)} collective-permute-done((bf16[4,32,2048]{2,1,0:T(8,128)(2,1)}, bf16[4,32,2048]{2,1,0:T(8,128)(2,1)S(1)}, u32[]{:S(2)}, u32[]{:S(2)}) %collective-permute-start.19) | collective-permute-done | bytes 524320 | tf_op jit(solution)/shard_map/ppermute | solution.py:31
  100.4 3.1 %collective-permute-start.28 = (bf16[4,32,2048]{2,1,0:T(8,128)(2,1)}, bf16[4,32,2048]{2,1,0:T(8,128)(2,1)}, u32[]{:S(2)}, u32[]{:S(2)}) collective-permute-start(bf16[4,32,2048]{2,1,0:T(8,128)(2,1)} %get-tuple-element.49), channel_id=1, source_target_pairs={{0,24},{8,0},{16,8},{24,16},{32,56},{40,32},{48,40},{56,48},{64,88... | collective-permute-start | bytes 1572872 | tf_op jit(solution)/shard_map/ppermute | solution.py:31
  103.6 2.8 %collective-permute-start.30 = (bf16[4,32,2048]{2,1,0:T(8,128)(2,1)}, bf16[4,32,2048]{2,1,0:T(8,128)(2,1)}, u32[]{:S(2)}, u32[]{:S(2)}) collective-permute-start(bf16[4,32,2048]{2,1,0:T(8,128)(2,1)} %get-tuple-element.52), channel_id=1, source_target_pairs={{0,64},{8,72},{16,80},{24,88},{32,96},{40,104},{48,112},{56,120},{... | collective-permute-start | bytes 1572872 | tf_op jit(solution)/shard_map/ppermute | solution.py:26
  106.3 4.2 %collective-permute-done.26.refs_10_ = bf16[4,32,2048]{2,1,0:T(8,128)(2,1)S(1)} collective-permute-done((bf16[4,32,2048]{2,1,0:T(8,128)(2,1)}, bf16[4,32,2048]{2,1,0:T(8,128)(2,1)S(1)}, u32[]{:S(2)}, u32[]{:S(2)}) %collective-permute-start.26) | collective-permute-done | bytes 524320 | tf_op jit(solution)/shard_map/ppermute | solution.py:31
  111.9 18.6 %shard_map.47 = (f32[48,32,128]{2,1,0:T(8,128)}, s16[1584,128]{1,0:T(8,128)(2,1)}, s16[1584,128]{1,0:T(8,128)(2,1)}, s16[1584,128]{1,0:T(8,128)(2,1)}) custom-call(s32[9]{0:T(128)} %broadcast_add_fusion.refs_0_, s32[4]{0:T(128)} %copy-done.23, s32[36]{0:T(128)} %get-tuple-element.82.refs_2_, s32[36]{0:T(128)} %get-tuple-element.81.refs_3_, ...), custom_call_target="tpu_custom_call" | custom-call | tf_op jit(solution)/shard_map/pallas_call | solution.py:200
  131.9 2.6 %collective-permute-start.24 = (s16[1584,128]{1,0:T(8,128)(2,1)}, s16[1584,128]{1,0:T(8,128)(2,1)S(1)}, u32[]{:S(2)}, u32[]{:S(2)}) collective-permute-start(s16[1584,128]{1,0:T(8,128)(2,1)} %get-tuple-element.43), channel_id=1, source_target_pairs={{0,4},{1,5},{2,6},{3,7},{4,0},{5,1},{6,2},{7,3},{8,12},{9,13},{10,... | collective-permute-start | bytes 1216520 | tf_op jit(solution)/shard_map/ppermute | solution.py:36
  135.6 18.5 %shard_map.49 = (f32[48,32,128]{2,1,0:T(8,128)}, s16[1584,128]{1,0:T(8,128)(2,1)}, s16[1584,128]{1,0:T(8,128)(2,1)}, s16[1584,128]{1,0:T(8,128)(2,1)}) custom-call(s32[9]{0:T(128)} %broadcast_add_fusion.refs_0_, s32[4]{0:T(128)} %copy-done.23, s32[36]{0:T(128)} %get-tuple-element.82.refs_2_, s32[36]{0:T(128)} %get-tuple-element.81.refs_3_, ...), custom_call_target="tpu_custom_call" | custom-call | tf_op jit(solution)/shard_map/pallas_call | solution.py:200
  158.1 3.5 %finish.2 = (f32[24,32,64]{2,1,0:T(8,128)}, f32[24,32,64]{2,1,0:T(8,128)}) custom-call(f32[48,32,128]{2,1,0:T(8,128)} %get-tuple-element.41.kept, s16[1584,128]{1,0:T(8,128)(2,1)} %copy-done.14, s16[1584,128]{1,0:T(8,128)(2,1)} %copy-done.15, s16[1584,128]{1,0:T(8,128)(2,1)} %copy-done.16), custom_call_target="tpu_custom_call" | custom-call | tf_op jit(solution)/shard_map/finish/pallas_call | solution.py:236
  161.6 15.0 %collective-permute-start.35 = (f32[24,32,64]{2,1,0:T(8,128)}, f32[24,32,64]{2,1,0:T(8,128)S(1)}, u32[]{:S(2)}, u32[]{:S(2)}) collective-permute-start(f32[24,32,64]{2,1,0:T(8,128)} %get-tuple-element.59), channel_id=1, source_target_pairs={{0,1},{1,0},{2,3},{3,2},{4,5},{5,4},{6,7},{7,6},{8,9},{9,8},{10,11... | collective-permute-start | bytes 589832 | tf_op jit(solution)/shard_map/ppermute | solution.py:40
  177.7 3.5 %finish.3 = (f32[24,32,64]{2,1,0:T(8,128)}, f32[24,32,64]{2,1,0:T(8,128)}) custom-call(f32[48,32,128]{2,1,0:T(8,128)} %get-tuple-element.54.kept, s16[1584,128]{1,0:T(8,128)(2,1)} %copy-done.17, s16[1584,128]{1,0:T(8,128)(2,1)} %copy-done.18, s16[1584,128]{1,0:T(8,128)(2,1)} %copy-done.19), custom_call_target="tpu_custom_call" | custom-call | tf_op jit(solution)/shard_map/finish/pallas_call | solution.py:236
  181.2 6.3 %collective-permute-start.36 = (f32[24,32,64]{2,1,0:T(8,128)}, f32[24,32,64]{2,1,0:T(8,128)S(1)}, u32[]{:S(2)}, u32[]{:S(2)}) collective-permute-start(f32[24,32,64]{2,1,0:T(8,128)} %get-tuple-element.60), channel_id=1, source_target_pairs={{0,1},{1,0},{2,3},{3,2},{4,5},{5,4},{6,7},{7,6},{8,9},{9,8},{10,11... | collective-permute-start | bytes 589832 | tf_op jit(solution)/shard_map/ppermute | solution.py:40
  (142 shorter events, 40.8 us)
Async XLA Ops:
  5.7 27.2 %collective-permute-start.13 = (bf16[4,64,2048]{2,1,0:T(8,128)(2,1)S(1)}, bf16[4,64,2048]{2,1,0:T(8,128)(2,1)S(1)}, u32[]{:S(2)}, u32[]{:S(2)}) collective-permute-start(bf16[4,64,2048]{2,1,0:T(8,128)(2,1)S(1)} %fusion.3.refs_13_.refs_18_), channel_id=1, source_target_pairs={{0,8},{8,16},{16,24},{24,0},{32,40},{40,48},{48,56},{56,32},{64,72... | collective-permute-start | bytes 3145736 | tf_op jit(solution)/shard_map/ppermute | solution.py:31
  7.5 26.3 %collective-permute-start.14 = (bf16[4,64,2048]{2,1,0:T(8,128)(2,1)S(1)}, bf16[4,64,2048]{2,1,0:T(8,128)(2,1)}, u32[]{:S(2)}, u32[]{:S(2)}) collective-permute-start(bf16[4,64,2048]{2,1,0:T(8,128)(2,1)S(1)} %fusion.3.refs_13_.refs_18_), channel_id=1, source_target_pairs={{0,24},{8,0},{16,8},{24,16},{32,56},{40,32},{48,40},{56,48},{64,88... | collective-permute-start | bytes 3145736 | tf_op jit(solution)/shard_map/ppermute | solution.py:31
  9.8 25.4 %collective-permute-start.9 = (bf16[4,64,2048]{2,1,0:T(8,128)(2,1)S(1)}, bf16[4,64,2048]{2,1,0:T(8,128)(2,1)}, u32[]{:S(2)}, u32[]{:S(2)}) collective-permute-start(bf16[4,64,2048]{2,1,0:T(8,128)(2,1)S(1)} %pad_maximum_fusion.refs_8_.refs_13_), channel_id=1, source_target_pairs={{0,32},{8,40},{16,48},{24,56},{32,64},{40,72},{48,80},{56,88},{64,... | collective-permute-start | bytes 3145736 | tf_op jit(solution)/shard_map/ppermute | solution.py:26
  11.1 27.9 %collective-permute-start.10 = (bf16[4,64,2048]{2,1,0:T(8,128)(2,1)S(1)}, bf16[4,64,2048]{2,1,0:T(8,128)(2,1)}, u32[]{:S(2)}, u32[]{:S(2)}) collective-permute-start(bf16[4,64,2048]{2,1,0:T(8,128)(2,1)S(1)} %pad_maximum_fusion.refs_8_.refs_13_), channel_id=1, source_target_pairs={{0,96},{8,104},{16,112},{24,120},{32,0},{40,8},{48,16},{56,24},{64... | collective-permute-start | bytes 3145736 | tf_op jit(solution)/shard_map/ppermute | solution.py:26
  12.6 69.2 %collective-permute-start = (bf16[1024,1024]{1,0:T(8,128)(2,1)}, bf16[1024,1024]{1,0:T(8,128)(2,1)}, u32[]{:S(2)}, u32[]{:S(2)}) collective-permute-start(bf16[1024,1024]{1,0:T(8,128)(2,1)} %param.4), channel_id=1, source_target_pairs={{0,1},{1,0},{2,3},{3,2},{4,5},{5,4},{6,7},{7,6},{8,9},{9,8},{10,11... | collective-permute-start | bytes 6291464 | tf_op jit(solution)/shard_map/ppermute | solution.py:40
  32.9 48.9 %collective-permute-start.1 = (bf16[1024,1024]{1,0:T(8,128)(2,1)}, bf16[1024,1024]{1,0:T(8,128)(2,1)}, u32[]{:S(2)}, u32[]{:S(2)}) collective-permute-start(bf16[1024,1024]{1,0:T(8,128)(2,1)} %param.5), channel_id=1, source_target_pairs={{0,1},{1,0},{2,3},{3,2},{4,5},{5,4},{6,7},{7,6},{8,9},{9,8},{10,11... | collective-permute-start | bytes 6291464 | tf_op jit(solution)/shard_map/ppermute | solution.py:40
  33.8 21.3 %collective-permute-start.15 = (bf16[2,64,2048]{2,1,0:T(8,128)(2,1)S(1)}, bf16[2,64,2048]{2,1,0:T(8,128)(2,1)}, u32[]{:S(2)}, u32[]{:S(2)}) collective-permute-start(bf16[2,64,2048]{2,1,0:T(8,128)(2,1)S(1)} %slice.48), channel_id=1, source_target_pairs={{0,8},{8,16},{16,24},{24,0},{32,40},{40,48},{48,56},{56,32},{64,72... | collective-permute-start | bytes 1572872 | tf_op jit(solution)/shard_map/ppermute | solution.py:31
  73.3 19.0 %collective-permute-start.18 = (bf16[4,32,2048]{2,1,0:T(8,128)(2,1)}, bf16[4,32,2048]{2,1,0:T(8,128)(2,1)S(1)}, u32[]{:S(2)}, u32[]{:S(2)}) collective-permute-start(bf16[4,32,2048]{2,1,0:T(8,128)(2,1)} %get-tuple-element.35), channel_id=1, source_target_pairs={{0,16},{8,24},{16,0},{24,8},{32,48},{40,56},{48,32},{56,40},{64,80... | collective-permute-start | bytes 1572872 | tf_op jit(solution)/shard_map/ppermute | solution.py:31
  73.8 25.7 %collective-permute-start.19 = (bf16[4,32,2048]{2,1,0:T(8,128)(2,1)}, bf16[4,32,2048]{2,1,0:T(8,128)(2,1)S(1)}, u32[]{:S(2)}, u32[]{:S(2)}) collective-permute-start(bf16[4,32,2048]{2,1,0:T(8,128)(2,1)} %get-tuple-element.36), channel_id=1, source_target_pairs={{0,24},{8,0},{16,8},{24,16},{32,56},{40,32},{48,40},{56,48},{64,88... | collective-permute-start | bytes 1572872 | tf_op jit(solution)/shard_map/ppermute | solution.py:31
  81.7 18.7 %collective-permute-start.20 = (bf16[4,32,2048]{2,1,0:T(8,128)(2,1)}, bf16[4,32,2048]{2,1,0:T(8,128)(2,1)S(1)}, u32[]{:S(2)}, u32[]{:S(2)}) collective-permute-start(bf16[4,32,2048]{2,1,0:T(8,128)(2,1)} %get-tuple-element.38), channel_id=1, source_target_pairs={{0,32},{8,40},{16,48},{24,56},{32,64},{40,72},{48,80},{56,88},{64,... | collective-permute-start | bytes 1572872 | tf_op jit(solution)/shard_map/ppermute | solution.py:26
  81.8 21.7 %collective-permute-start.21 = (bf16[4,32,2048]{2,1,0:T(8,128)(2,1)}, bf16[4,32,2048]{2,1,0:T(8,128)(2,1)S(1)}, u32[]{:S(2)}, u32[]{:S(2)}) collective-permute-start(bf16[4,32,2048]{2,1,0:T(8,128)(2,1)} %get-tuple-element.39), channel_id=1, source_target_pairs={{0,64},{8,72},{16,80},{24,88},{32,96},{40,104},{48,112},{56,120},{... | collective-permute-start | bytes 1572872 | tf_op jit(solution)/shard_map/ppermute | solution.py:26
  92.3 18.2 %collective-permute-start.26 = (bf16[4,32,2048]{2,1,0:T(8,128)(2,1)}, bf16[4,32,2048]{2,1,0:T(8,128)(2,1)S(1)}, u32[]{:S(2)}, u32[]{:S(2)}) collective-permute-start(bf16[4,32,2048]{2,1,0:T(8,128)(2,1)} %get-tuple-element.47), channel_id=1, source_target_pairs={{0,8},{8,16},{16,24},{24,0},{32,40},{40,48},{48,56},{56,32},{64,72... | collective-permute-start | bytes 1572872 | tf_op jit(solution)/shard_map/ppermute | solution.py:31
  99.5 31.1 %collective-permute-start.27 = (bf16[4,32,2048]{2,1,0:T(8,128)(2,1)}, bf16[4,32,2048]{2,1,0:T(8,128)(2,1)S(1)}, u32[]{:S(2)}, u32[]{:S(2)}) collective-permute-start(bf16[4,32,2048]{2,1,0:T(8,128)(2,1)} %get-tuple-element.48), channel_id=1, source_target_pairs={{0,16},{8,24},{16,0},{24,8},{32,48},{40,56},{48,32},{56,40},{64,80... | collective-permute-start | bytes 1572872 | tf_op jit(solution)/shard_map/ppermute | solution.py:31
  100.4 31.5 %collective-permute-start.28 = (bf16[4,32,2048]{2,1,0:T(8,128)(2,1)}, bf16[4,32,2048]{2,1,0:T(8,128)(2,1)}, u32[]{:S(2)}, u32[]{:S(2)}) collective-permute-start(bf16[4,32,2048]{2,1,0:T(8,128)(2,1)} %get-tuple-element.49), channel_id=1, source_target_pairs={{0,24},{8,0},{16,8},{24,16},{32,56},{40,32},{48,40},{56,48},{64,88... | collective-permute-start | bytes 1572872 | tf_op jit(solution)/shard_map/ppermute | solution.py:31
  103.5 31.0 %collective-permute-start.29 = (bf16[4,32,2048]{2,1,0:T(8,128)(2,1)}, bf16[4,32,2048]{2,1,0:T(8,128)(2,1)}, u32[]{:S(2)}, u32[]{:S(2)}) collective-permute-start(bf16[4,32,2048]{2,1,0:T(8,128)(2,1)} %get-tuple-element.51), channel_id=1, source_target_pairs={{0,32},{8,40},{16,48},{24,56},{32,64},{40,72},{48,80},{56,88},{64,... | collective-permute-start | bytes 1572872 | tf_op jit(solution)/shard_map/ppermute | solution.py:26
  103.6 32.1 %collective-permute-start.30 = (bf16[4,32,2048]{2,1,0:T(8,128)(2,1)}, bf16[4,32,2048]{2,1,0:T(8,128)(2,1)}, u32[]{:S(2)}, u32[]{:S(2)}) collective-permute-start(bf16[4,32,2048]{2,1,0:T(8,128)(2,1)} %get-tuple-element.52), channel_id=1, source_target_pairs={{0,64},{8,72},{16,80},{24,88},{32,96},{40,104},{48,112},{56,120},{... | collective-permute-start | bytes 1572872 | tf_op jit(solution)/shard_map/ppermute | solution.py:26
  110.5 25.1 %collective-permute-start.31 = (bf16[4,32,2048]{2,1,0:T(8,128)(2,1)}, bf16[4,32,2048]{2,1,0:T(8,128)(2,1)}, u32[]{:S(2)}, u32[]{:S(2)}) collective-permute-start(bf16[4,32,2048]{2,1,0:T(8,128)(2,1)} %get-tuple-element.53), channel_id=1, source_target_pairs={{0,96},{8,104},{16,112},{24,120},{32,0},{40,8},{48,16},{56,24},{64... | collective-permute-start | bytes 1572872 | tf_op jit(solution)/shard_map/ppermute | solution.py:26
  130.5 24.9 %collective-permute-start.23 = (s16[1584,128]{1,0:T(8,128)(2,1)}, s16[1584,128]{1,0:T(8,128)(2,1)S(1)}, u32[]{:S(2)}, u32[]{:S(2)}) collective-permute-start(s16[1584,128]{1,0:T(8,128)(2,1)} %get-tuple-element.42), channel_id=1, source_target_pairs={{0,2},{1,3},{2,4},{3,5},{4,6},{5,7},{6,0},{7,1},{8,10},{9,11},{10,... | collective-permute-start | bytes 1216520 | tf_op jit(solution)/shard_map/ppermute | solution.py:36
  131.9 25.2 %collective-permute-start.24 = (s16[1584,128]{1,0:T(8,128)(2,1)}, s16[1584,128]{1,0:T(8,128)(2,1)S(1)}, u32[]{:S(2)}, u32[]{:S(2)}) collective-permute-start(s16[1584,128]{1,0:T(8,128)(2,1)} %get-tuple-element.43), channel_id=1, source_target_pairs={{0,4},{1,5},{2,6},{3,7},{4,0},{5,1},{6,2},{7,3},{8,12},{9,13},{10,... | collective-permute-start | bytes 1216520 | tf_op jit(solution)/shard_map/ppermute | solution.py:36
  134.5 22.6 %collective-permute-start.25 = (s16[1584,128]{1,0:T(8,128)(2,1)}, s16[1584,128]{1,0:T(8,128)(2,1)S(1)}, u32[]{:S(2)}, u32[]{:S(2)}) collective-permute-start(s16[1584,128]{1,0:T(8,128)(2,1)} %get-tuple-element.44), channel_id=1, source_target_pairs={{0,6},{1,7},{2,0},{3,1},{4,2},{5,3},{6,4},{7,5},{8,14},{9,15},{10,... | collective-permute-start | bytes 1216520 | tf_op jit(solution)/shard_map/ppermute | solution.py:36
  154.2 22.5 %collective-permute-start.32 = (s16[1584,128]{1,0:T(8,128)(2,1)}, s16[1584,128]{1,0:T(8,128)(2,1)S(1)}, u32[]{:S(2)}, u32[]{:S(2)}) collective-permute-start(s16[1584,128]{1,0:T(8,128)(2,1)} %get-tuple-element.55), channel_id=1, source_target_pairs={{0,2},{1,3},{2,4},{3,5},{4,6},{5,7},{6,0},{7,1},{8,10},{9,11},{10,... | collective-permute-start | bytes 1216520 | tf_op jit(solution)/shard_map/ppermute | solution.py:36
  154.6 22.0 %collective-permute-start.33 = (s16[1584,128]{1,0:T(8,128)(2,1)}, s16[1584,128]{1,0:T(8,128)(2,1)S(1)}, u32[]{:S(2)}, u32[]{:S(2)}) collective-permute-start(s16[1584,128]{1,0:T(8,128)(2,1)} %get-tuple-element.56), channel_id=1, source_target_pairs={{0,4},{1,5},{2,6},{3,7},{4,0},{5,1},{6,2},{7,3},{8,12},{9,13},{10,... | collective-permute-start | bytes 1216520 | tf_op jit(solution)/shard_map/ppermute | solution.py:36
  155.4 21.2 %collective-permute-start.34 = (s16[1584,128]{1,0:T(8,128)(2,1)}, s16[1584,128]{1,0:T(8,128)(2,1)S(1)}, u32[]{:S(2)}, u32[]{:S(2)}) collective-permute-start(s16[1584,128]{1,0:T(8,128)(2,1)} %get-tuple-element.57), channel_id=1, source_target_pairs={{0,6},{1,7},{2,0},{3,1},{4,2},{5,3},{6,4},{7,5},{8,14},{9,15},{10,... | collective-permute-start | bytes 1216520 | tf_op jit(solution)/shard_map/ppermute | solution.py:36
  161.6 25.9 %collective-permute-start.35 = (f32[24,32,64]{2,1,0:T(8,128)}, f32[24,32,64]{2,1,0:T(8,128)S(1)}, u32[]{:S(2)}, u32[]{:S(2)}) collective-permute-start(f32[24,32,64]{2,1,0:T(8,128)} %get-tuple-element.59), channel_id=1, source_target_pairs={{0,1},{1,0},{2,3},{3,2},{4,5},{5,4},{6,7},{7,6},{8,9},{9,8},{10,11... | collective-permute-start | bytes 589832 | tf_op jit(solution)/shard_map/ppermute | solution.py:40
  (43 other events, 508.4 us)
where the time goes:
time: 192 us; the launch traced here: 191 us
  starting transfers between devices  63.4 us (33%)
  waiting for transfers between devices  59.6 us (31%)
  Pallas kernels  54.8 us (29%)
  local copies, waits for them, and re-layouts  8.55 us (4%)
  other arithmetic  4.51 us (2%)
    ppermute x13, waiting for transfers between devices, shift_z(): return lax.ppermute(value, 'row', perm)  49.2 us
    pallas_call x2, Pallas kernels, products(): pl.pallas_call(functools.partial(product_kernel, offset, rows, slots), ou...  37.2 us
    ppermute x5, starting transfers between devices, swap_cores(): return lax.ppermute(value, 'col', [(c, c ^ 1) for c in range(SIDE * 2)])  24.8 us
    ppermute x13, starting transfers between devices, shift_x(): return lax.ppermute(value, 'row', perm)  16.5 us
    ppermute x13, starting transfers between devices, shift_z(): return lax.ppermute(value, 'row', perm)  14 us
    pallas_call x2, Pallas kernels, pick(): pl.pallas_call(functools.partial(pick_kernel, offset), out_shape=[piece]...  10.6 us
    ppermute x6, starting transfers between devices, shift_y(): return lax.ppermute(value, 'col', perm)  8.02 us
    pallas_call x2, Pallas kernels, finish(): pl.pallas_call(finish_kernel, grid=(steps,), out_shape=[jax.ShapeDtypeStr...  7.07 us
  transfers between devices with their start and end apart: 37, of which 13 were waited for; matrix products, arithmetic and copies ran while one was open for 3% of the time, Pallas kernels for 29%

commit v1 on v0

--- a/solution.py
+++ b/solution.py
@@ -19,6 +19,7 @@
 ANY = pl.BlockSpec(memory_space=pl.ANY)
 SMEM = pl.BlockSpec(memory_space=pltpu.SMEM)
 VMEM = pl.BlockSpec(memory_space=pltpu.VMEM)
+LEFT = pl.BlockSpec(memory_space=pltpu.VMEM)
 
 
 def shift_x(value, step):
@@ -85,6 +86,7 @@
         in_specs=[SMEM] * 8 + [ANY] * 10,
         out_specs=[VMEM] * 8,
         scratch_shapes=[pltpu.SemaphoreType.DMA((2, SIDE, SIDE))],
+        compiler_params=pltpu.CompilerParams(vmem_limit_bytes=16 << 20),
     )(*wants_z, *wants_x, *held_a, *held_b)
     return outs[:4], outs[4:]
 
@@ -99,17 +101,15 @@
     out[pl.ds(count * ROWS, count)] = level.astype(jnp.int32).astype(jnp.int16)
 
 
-def product_kernel(offset, rows, slots, *refs):
-    group_first, group_start, slot_tile, slot_a, slot_b = refs[0:5]
-    lefts = refs[5:9]
-    tables = (refs[9:14], refs[14:19])
-    kept, coded = refs[19], refs[20:23]
-    left, held_a, held_b, acc, sems, left_sems, out_sem = refs[23:]
+def product_kernel(offset, rows, slots, lists, left, *refs):
+    tables = (refs[0:5], refs[5:10])
+    kept, coded = refs[10], refs[11:14]
+    held_a, held_b, acc, sems, out_sem = refs[14:]
     y = lax.axis_index("col") // 2
-    features = lefts[0].shape[2]
     width = 2 * rows
     group = TILE // width
     blocks = kept.shape[0]
+    places = slots * group
     copies = []
     for half, held in enumerate((held_a, held_b)):
         for place in range(5):
@@ -119,34 +119,24 @@
             copies.append(
                 pltpu.make_async_copy(source, held.at[pl.ds(place * SIDE, SIDE)], sems.at[half, place])
             )
-    left_copies = []
-    for block in range(SIDE):
-        for n in range(4):
-            target = left.at[block, pl.ds(n % 2 * TILE, TILE), pl.ds(n // 2 * features, features)]
-            left_copies.append(pltpu.make_async_copy(lefts[n].at[block], target, left_sems.at[block, n]))
-    for copy in copies + left_copies:
+    for copy in copies:
         copy.start()
     for copy in copies:
         copy.wait()
 
     def one(slot, carry):
-        for block in range(SIDE):
-            @pl.when(group_start[block] == slot)
-            def _():
-                for copy in left_copies[4 * block : 4 * block + 4]:
-                    copy.wait()
-
         right = []
         for g in range(group):
-            right += [held_a[slot_a[slot * group + g]], held_b[slot_b[slot * group + g]]]
+            place = slots + slot * group + g
+            right += [held_a[lists[place + places]], held_b[lists[place + 2 * places]]]
         out = lax.dot_general(
-            left[group_first[slot]],
+            left[lists[slot]],
             jnp.concatenate(right, axis=0),
             (((1,), (1,)), ((), ())),
             preferred_element_type=jnp.float32,
         )
         for g in range(group):
-            tile = slot_tile[slot * group + g]
+            tile = lists[slots + slot * group + g]
             cross_x = out[:TILE, g * width : (g + 1) * width]
             cross_s = out[TILE:, g * width : (g + 1) * width]
             parts = jnp.concatenate([cross_x, cross_s], axis=1).reshape(SIDE, 2, ROWS, LANES)
@@ -156,12 +146,6 @@
         return carry
 
     lax.fori_loop(0, slots, one, 0, unroll=3)
-    for block in range(SIDE):
-        @pl.when(group_start[block] >= slots)
-        def _():
-            for copy in left_copies[4 * block : 4 * block + 4]:
-                copy.wait()
-
     keep = pltpu.make_async_copy(acc.at[0, pl.ds(0, blocks)], kept, out_sem)
     keep.start()
     for d in range(1, SIDE):
@@ -190,32 +174,31 @@
     slot_b = jnp.where(used, pull(spot_b), 16)
     past = jnp.arange(slots, dtype=jnp.int32)[:, None] >= starts[None, :]
     group_first = jnp.sum(jnp.where(past, 1, 0), axis=1) - 1
-    return slots, (group_first, starts, slot_tile, slot_a, slot_b)
-
-
-def products(lists, slots, lefts, table_a, table_b, offset, rows, tiles):
-    features = 2 * lefts[0].shape[2]
+    return slots, jnp.concatenate([group_first, slot_tile, slot_a, slot_b])
+
+
+def products(lists, slots, left, table_a, table_b, offset, rows, tiles):
+    features = left.shape[2]
     blocks = 2 * tiles
     code = jax.ShapeDtypeStruct((blocks // 16 * LENGTH, LANES), jnp.int16)
     return pl.pallas_call(
         functools.partial(product_kernel, offset, rows, slots),
         out_shape=[jax.ShapeDtypeStruct((blocks, ROWS, LANES), jnp.float32)] + [code] * 3,
-        in_specs=[SMEM] * 5 + [ANY] * 14,
+        in_specs=[SMEM] + [LEFT] + [ANY] * 10,
         out_specs=[ANY] + [VMEM] * 3,
         scratch_shapes=[
-            pltpu.VMEM((SIDE, 2 * TILE, features), jnp.bfloat16),
             pltpu.VMEM((20, rows, features), jnp.bfloat16),
             pltpu.VMEM((20, rows, features), jnp.bfloat16),
             pltpu.VMEM((SIDE, blocks + 2, ROWS, LANES), jnp.float32),
             pltpu.SemaphoreType.DMA((2, 5)),
-            pltpu.SemaphoreType.DMA((SIDE, 4)),
             pltpu.SemaphoreType.DMA,
         ],
-    )(*lists, *lefts, *table_a, *table_b)
-
-
-def finish_kernel(kept, *refs):
-    coded, mine, theirs = refs[:3], refs[3], refs[4]
+        compiler_params=pltpu.CompilerParams(vmem_limit_bytes=28 << 20),
+    )(lists, pltpu.with_memory_space_constraint(left, pltpu.VMEM), *table_a, *table_b)
+
+
+def finish_kernel(before, kept, *refs):
+    coded, earlier, mine, theirs = refs[:3], refs[3 : 3 + 2 * before], refs[-2], refs[-1]
     core = lax.axis_index("col") % 2
     count = kept.shape[0]
     total = kept[...]
@@ -225,23 +208,33 @@
         factor = jnp.exp2(level * (1.0 / 256.0)) * (1.0 / TOP)
         total = total + code.reshape(count, ROWS, LANES) * factor[:, None, :]
     pairs = (total[..., : LANES // 2] * total[..., LANES // 2 :]).reshape(count // 2, 2, ROWS, LANES // 2)
-    mine[...] = jnp.where(core == 0, pairs[:, 0], pairs[:, 1])
-    theirs[...] = jnp.where(core == 0, pairs[:, 1], pairs[:, 0])
-
-
-def finish(kept, coded):
+    first = jnp.where(core == 0, pairs[:, 0], pairs[:, 1])
+    second = jnp.where(core == 0, pairs[:, 1], pairs[:, 0])
+    if before:
+        first = jnp.concatenate([earlier[0][...], first], axis=-1)
+        second = jnp.concatenate([earlier[1][...], second], axis=-1)
+    mine[...] = first
+    theirs[...] = second
+
+
+def finish(kept, coded, earlier):
     blocks = kept.shape[0]
     steps = blocks // 16
-    out_block = pl.BlockSpec((8, ROWS, LANES // 2), lambda s: (s, 0, 0))
+    before = 1 if earlier else 0
+    lanes = LANES // 2 * (1 + before)
+    half_block = pl.BlockSpec((8, ROWS, LANES // 2), lambda s: (s, 0, 0))
+    out_block = pl.BlockSpec((8, ROWS, lanes), lambda s: (s, 0, 0))
     return pl.pallas_call(
-        finish_kernel,
+        functools.partial(finish_kernel, before),
         grid=(steps,),
-        out_shape=[jax.ShapeDtypeStruct((8 * steps, ROWS, LANES // 2), jnp.float32)] * 2,
+        out_shape=[jax.ShapeDtypeStruct((8 * steps, ROWS, lanes), jnp.float32)] * 2,
         in_specs=[pl.BlockSpec((16, ROWS, LANES), lambda s: (s, 0, 0))]
-        + [pl.BlockSpec((LENGTH, LANES), lambda s: (s, 0))] * 3,
+        + [pl.BlockSpec((LENGTH, LANES), lambda s: (s, 0))] * 3
+        + [half_block] * (2 * before),
         out_specs=[out_block, out_block],
+        compiler_params=pltpu.CompilerParams(vmem_limit_bytes=16 << 20),
         name="finish",
-    )(kept, *coded)
+    )(kept, *coded, *earlier)
 
 
 def gather_ring(own, shift):
@@ -270,8 +263,10 @@
     half_b = [owned[:, s + w // 2 : s + w] for s, w in zip(starts, WIDTHS)]
     held_a = gather_ring(jnp.concatenate(half_a, axis=1), shift_x)
     held_b = gather_ring(jnp.concatenate(half_b, axis=1), shift_z)
-    lefts = [primal_rows, dual_rows, swap_cores(primal_rows), swap_cores(dual_rows)]
-    lefts = [v.reshape(blocks, TILE, features) for v in lefts]
+    own = [v.reshape(blocks, TILE, features) for v in (primal_rows, dual_rows)]
+    other = [swap_cores(v) for v in (primal_rows, dual_rows)]
+    other = [v.reshape(blocks, TILE, features) for v in other]
+    left = jnp.concatenate([jnp.concatenate(own, axis=1), jnp.concatenate(other, axis=1)], axis=2)
 
     second = pairs[:, 1]
     owner, local = second // blocks, second % blocks
@@ -294,14 +289,11 @@
     outs = []
     for (table_a, table_b), start, width in zip(arrived, starts, WIDTHS):
         slots, lists = grouped(first, spot_a, spot_b, TILE // width)
-        kept, *coded = products(
-            lists, slots, lefts, table_a, table_b, start // 2, width // 2, tiles
-        )
+        kept, *coded = products(lists, slots, left, table_a, table_b, start // 2, width // 2, tiles)
         moved = [shift_y(code, d + 1) for d, code in enumerate(coded)]
-        mine, theirs = finish(kept, moved)
-        outs.append((mine, swap_cores(theirs)))
-    mine = jnp.concatenate([m for m, _ in outs], axis=-1)
-    theirs = jnp.concatenate([t for _, t in outs], axis=-1)
+        outs = finish(kept, moved, outs)
+    mine, theirs = outs
+    theirs = swap_cores(theirs)
     low = jnp.where(core == 0, mine, theirs)
     high = jnp.where(core == 0, theirs, mine)
     return jnp.concatenate([low, high], axis=-1)

time: 192 us -> 196 us (1.021)
  the two profiles are of different devices: /device:TPU:1 before, /device:TPU:11 now
where the time goes in v1:
time: 196 us
  waiting for transfers between devices  105 us (54%)
  starting transfers between devices  49 us (25%)
  Pallas kernels  31.1 us (16%)
  other arithmetic  8.71 us (4%)
    ppermute x13, waiting for transfers between devices, shift_z(): return lax.ppermute(value, 'row', perm)  39.5 us
    ppermute x6, waiting for transfers between devices, shift_y(): return lax.ppermute(value, 'col', perm)  31.8 us
    ppermute x13, waiting for transfers between devices, shift_x(): return lax.ppermute(value, 'row', perm)  30 us
    ppermute x13, starting transfers between devices, shift_z(): return lax.ppermute(value, 'row', perm)  24.3 us
    pallas_call x2, Pallas kernels, products(): pl.pallas_call(functools.partial(product_kernel, offset, rows, slots), ou...  16.3 us
    ppermute x13, starting transfers between devices, shift_x(): return lax.ppermute(value, 'row', perm)  14 us
    pallas_call x2, Pallas kernels, pick(): pl.pallas_call(functools.partial(pick_kernel, offset), out_shape=[piece]...  13.3 us
    ppermute x6, starting transfers between devices, shift_y(): return lax.ppermute(value, 'col', perm)  6.79 us
  transfers between devices with their start and end apart: 36, of which 16 were waited for; matrix products, arithmetic and copies ran while one was open for 3% of the time, Pallas kernels for 15%

profile of v1, /device:TPU:11, one launch (start us, length us, event | category | flops | bytes accessed | tf_op | source)
XLA Modules:
  0.0 195.9 jit_solution(4196310054235862651)
XLA Ops:
  2.5 2.3 %collective-permute-done.8 = bf16[4,128,1024]{2,1,0:T(8,128)(2,1)S(1)} collective-permute-done((bf16[4,128,1024]{2,1,0:T(8,128)(2,1)S(1)}, bf16[4,128,1024]{2,1,0:T(8,128)(2,1)S(1)}, u32[]{:S(2)}, u32[]{:S(2)}) %collective-permute-start.8) | collective-permute-done | bytes 1048608 | tf_op jit(solution)/shard_map/ppermute | solution.py:41
  11.6 18.8 %collective-permute-done.9.refs_9_ = bf16[4,64,2048]{2,1,0:T(8,128)(2,1)S(1)} collective-permute-done((bf16[4,64,2048]{2,1,0:T(8,128)(2,1)S(1)}, bf16[4,64,2048]{2,1,0:T(8,128)(2,1)S(1)}, u32[]{:S(2)}, u32[]{:S(2)}) %collective-permute-start.9) | collective-permute-done | bytes 1048608 | tf_op jit(solution)/shard_map/ppermute | solution.py:27
  30.3 3.8 %collective-permute-start.14 = (bf16[4,64,2048]{2,1,0:T(8,128)(2,1)S(1)}, bf16[4,64,2048]{2,1,0:T(8,128)(2,1)S(1)}, u32[]{:S(2)}, u32[]{:S(2)}) collective-permute-start(bf16[4,64,2048]{2,1,0:T(8,128)(2,1)S(1)} %fusion.3.refs_13_.refs_9_), channel_id=1, source_target_pairs={{0,24},{8,0},{16,8},{24,16},{32,56},{40,32},{48,40},{56,48},{64,88... | collective-permute-start | bytes 3145736 | tf_op jit(solution)/shard_map/ppermute | solution.py:32
  37.9 17.4 %collective-permute-done.14.refs_15_ = bf16[4,64,2048]{2,1,0:T(8,128)(2,1)S(1)} collective-permute-done((bf16[4,64,2048]{2,1,0:T(8,128)(2,1)S(1)}, bf16[4,64,2048]{2,1,0:T(8,128)(2,1)S(1)}, u32[]{:S(2)}, u32[]{:S(2)}) %collective-permute-start.14) | collective-permute-done | bytes 1048608 | tf_op jit(solution)/shard_map/ppermute | solution.py:32
  55.4 2.0 %collective-permute-start.3 = (s32[16]{0:T(128)S(1)}, s32[16]{0:T(128)S(1)}, u32[]{:S(2)}, u32[]{:S(2)}) collective-permute-start(s32[16]{0:T(128)S(1)} %select_reduce_fusion.4.refs_0_.refs_4_), channel_id=1, source_target_pairs={{0,16},{8,24},{16,0},{24,8},{32,48},{40,56},{48,32},{56,40},{64,80... | collective-permute-start | bytes 200 | tf_op jit(solution)/shard_map/ppermute | solution.py:32
  57.5 2.0 %collective-permute-start.4 = (s32[16]{0:T(128)S(1)}, s32[16]{0:T(128)S(1)}, u32[]{:S(2)}, u32[]{:S(2)}) collective-permute-start(s32[16]{0:T(128)S(1)} %select_reduce_fusion.4.refs_0_.refs_4_), channel_id=1, source_target_pairs={{0,8},{8,16},{16,24},{24,0},{32,40},{40,48},{48,56},{56,32},{64,72... | collective-permute-start | bytes 200 | tf_op jit(solution)/shard_map/ppermute | solution.py:32
  67.3 2.1 %collective-permute-start.16 = (bf16[2,64,2048]{2,1,0:T(8,128)(2,1)S(1)}, bf16[2,64,2048]{2,1,0:T(8,128)(2,1)S(1)}, u32[]{:S(2)}, u32[]{:S(2)}) collective-permute-start(bf16[2,64,2048]{2,1,0:T(8,128)(2,1)S(1)} %slice.49), channel_id=1, source_target_pairs={{0,24},{8,0},{16,8},{24,16},{32,56},{40,32},{48,40},{56,48},{64,88... | collective-permute-start | bytes 1572872 | tf_op jit(solution)/shard_map/ppermute | solution.py:32
  69.8 4.1 %collective-permute-done.12.refs_12_ = bf16[2,64,2048]{2,1,0:T(8,128)(2,1)S(1)} collective-permute-done((bf16[2,64,2048]{2,1,0:T(8,128)(2,1)S(1)}, bf16[2,64,2048]{2,1,0:T(8,128)(2,1)S(1)}, u32[]{:S(2)}, u32[]{:S(2)}) %collective-permute-start.12) | collective-permute-done | bytes 524320 | tf_op jit(solution)/shard_map/ppermute | solution.py:27
  73.9 2.7 %collective-permute-done.15.refs_16_ = bf16[2,64,2048]{2,1,0:T(8,128)(2,1)S(1)} collective-permute-done((bf16[2,64,2048]{2,1,0:T(8,128)(2,1)S(1)}, bf16[2,64,2048]{2,1,0:T(8,128)(2,1)S(1)}, u32[]{:S(2)}, u32[]{:S(2)}) %collective-permute-start.15) | collective-permute-done | bytes 524320 | tf_op jit(solution)/shard_map/ppermute | solution.py:32
  76.6 6.6 %shard_map.46 = (bf16[4,32,2048]{2,1,0:T(8,128)(2,1)S(1)}, bf16[4,32,2048]{2,1,0:T(8,128)(2,1)S(1)}, bf16[4,32,2048]{2,1,0:T(8,128)(2,1)S(1)}, bf16[4,32,2048]{2...) custom-call(s32[16]{0:T(128)S(1)} %select_reduce_fusion.4.refs_0_.re, ...), custom_call_target="tpu_custom_call" | custom-call | tf_op jit(solution)/shard_map/pallas_call | solution.py:83
  84.0 6.6 %shard_map.48 = (bf16[4,32,2048]{2,1,0:T(8,128)(2,1)S(1)}, bf16[4,32,2048]{2,1,0:T(8,128)(2,1)S(1)}, bf16[4,32,2048]{2,1,0:T(8,128)(2,1)S(1)}, bf16[4,32,2048]{2...) custom-call(s32[16]{0:T(128)S(1)} %select_reduce_fusion.4.refs_0_.re, ...), custom_call_target="tpu_custom_call" | custom-call | tf_op jit(solution)/shard_map/pallas_call | solution.py:83
  96.4 2.2 %collective-permute-start.30 = (bf16[4,32,2048]{2,1,0:T(8,128)(2,1)S(1)}, bf16[4,32,2048]{2,1,0:T(8,128)(2,1)S(1)}, u32[]{:S(2)}, u32[]{:S(2)}) collective-permute-start(bf16[4,32,2048]{2,1,0:T(8,128)(2,1)S(1)} %get-tuple-element.51), channel_id=1, source_target_pairs={{0,64},{8,72},{16,80},{24,88},{32,96},{40,104},{48,112},{56,120},{... | collective-permute-start | bytes 1572872 | tf_op jit(solution)/shard_map/ppermute | solution.py:27
  98.6 7.3 %collective-permute-done.26.refs_1_ = bf16[4,32,2048]{2,1,0:T(8,128)(2,1)S(1)} collective-permute-done((bf16[4,32,2048]{2,1,0:T(8,128)(2,1)S(1)}, bf16[4,32,2048]{2,1,0:T(8,128)(2,1)S(1)}, u32[]{:S(2)}, u32[]{:S(2)}) %collective-permute-start.26) | collective-permute-done | bytes 524320 | tf_op jit(solution)/shard_map/ppermute | solution.py:32
  106.6 11.0 %collective-permute-done.27.refs_2_ = bf16[4,32,2048]{2,1,0:T(8,128)(2,1)S(1)} collective-permute-done((bf16[4,32,2048]{2,1,0:T(8,128)(2,1)S(1)}, bf16[4,32,2048]{2,1,0:T(8,128)(2,1)S(1)}, u32[]{:S(2)}, u32[]{:S(2)}) %collective-permute-start.27) | collective-permute-done | bytes 524320 | tf_op jit(solution)/shard_map/ppermute | solution.py:32
  118.7 3.6 %collective-permute-start.19 = (bf16[4,32,2048]{2,1,0:T(8,128)(2,1)S(1)}, bf16[4,32,2048]{2,1,0:T(8,128)(2,1)S(1)}, u32[]{:S(2)}, u32[]{:S(2)}) collective-permute-start(bf16[4,32,2048]{2,1,0:T(8,128)(2,1)S(1)} %get-tuple-element.36), channel_id=1, source_target_pairs={{0,24},{8,0},{16,8},{24,16},{32,56},{40,32},{48,40},{56,48},{64,88... | collective-permute-start | bytes 1572872 | tf_op jit(solution)/shard_map/ppermute | solution.py:32
  124.8 4.1 %maximum_maximum_fusion.left = bf16[4,512,2048]{2,1,0:T(8,128)(2,1)S(1)} fusion(bf16[4,256,1024]{2,1,0:T(8,128)(2,1)} %bitcast.6, bf16[4,256,1024]{2,1,0:T(8,128)(2,1)} %bitcast.5, bf16[4,256,1024]{2,1,0:T(8,128)(2,1)} %bitcast.4, bf16[4,256,1024]{2,1,0:T(8,128)(2,1)} %bitcast.3), kind=kLoop, calls=%fused_computation | loop fusion | flops 33554432 | bytes 16777216 | tf_op jit(solution)/shard_map/concatenate | solution.py:269
  129.0 8.1 %shard_map.49 = (f32[48,32,128]{2,1,0:T(8,128)S(1)}, s16[1584,128]{1,0:T(8,128)(2,1)S(1)}, s16[1584,128]{1,0:T(8,128)(2,1)S(1)}, s16[1584,128]{1,0:T(8,128)(2,1)S(1)}) custom-call(s32[117]{0:T(128)S(1)} %pad_add_fusion.lists, bf16[4,512,2048]{2,1,0:T(8,128)(2,1)S(1)} %maximum_maximum_fusion.left, bf16[4,32,2048]{2,1,0:T(8,128)(2,1)S(1)} %get-tuple-element.45.refs_0_, ...), custom_call_target="tpu_custom_call" | custom-call | tf_op jit(solution)/shard_map/pallas_call | solution.py:184
  138.5 5.8 %collective-permute-done.22.refs_8_ = bf16[4,32,2048]{2,1,0:T(8,128)(2,1)S(1)} collective-permute-done((bf16[4,32,2048]{2,1,0:T(8,128)(2,1)S(1)}, bf16[4,32,2048]{2,1,0:T(8,128)(2,1)S(1)}, u32[]{:S(2)}, u32[]{:S(2)}) %collective-permute-start.22) | collective-permute-done | bytes 524320 | tf_op jit(solution)/shard_map/ppermute | solution.py:27
  144.3 8.1 %shard_map.47 = (f32[48,32,128]{2,1,0:T(8,128)S(1)}, s16[1584,128]{1,0:T(8,128)(2,1)S(1)}, s16[1584,128]{1,0:T(8,128)(2,1)S(1)}, s16[1584,128]{1,0:T(8,128)(2,1)S(1)}) custom-call(s32[117]{0:T(128)S(1)} %pad_add_fusion.lists, bf16[4,512,2048]{2,1,0:T(8,128)(2,1)S(1)} %maximum_maximum_fusion.left, bf16[4,32,2048]{2,1,0:T(8,128)(2,1)S(1)} %get-tuple-element.33.refs_0_, ...), custom_call_target="tpu_custom_call" | custom-call | tf_op jit(solution)/shard_map/pallas_call | solution.py:184
  154.7 2.0 %collective-permute-start.34 = (s16[1584,128]{1,0:T(8,128)(2,1)S(1)}, s16[1584,128]{1,0:T(8,128)(2,1)S(1)}, u32[]{:S(2)}, u32[]{:S(2)}) collective-permute-start(s16[1584,128]{1,0:T(8,128)(2,1)S(1)} %get-tuple-element.56), channel_id=1, source_target_pairs={{0,6},{1,7},{2,0},{3,1},{4,2},{5,3},{6,4},{7,5},{8,14},{9,15},{10,... | collective-permute-start | bytes 1216520 | tf_op jit(solution)/shard_map/ppermute | solution.py:37
  157.9 4.3 %collective-permute-done.33.refs_1_ = s16[1584,128]{1,0:T(8,128)(2,1)S(1)} collective-permute-done((s16[1584,128]{1,0:T(8,128)(2,1)S(1)}, s16[1584,128]{1,0:T(8,128)(2,1)S(1)}, u32[]{:S(2)}, u32[]{:S(2)}) %collective-permute-start.33) | collective-permute-done | bytes 405536 | tf_op jit(solution)/shard_map/ppermute | solution.py:37
  162.2 14.2 %collective-permute-done.34.refs_2_ = s16[1584,128]{1,0:T(8,128)(2,1)S(1)} collective-permute-done((s16[1584,128]{1,0:T(8,128)(2,1)S(1)}, s16[1584,128]{1,0:T(8,128)(2,1)S(1)}, u32[]{:S(2)}, u32[]{:S(2)}) %collective-permute-start.34) | collective-permute-done | bytes 405536 | tf_op jit(solution)/shard_map/ppermute | solution.py:37
  178.0 12.4 %collective-permute-done.25.refs_2_ = s16[1584,128]{1,0:T(8,128)(2,1)S(1)} collective-permute-done((s16[1584,128]{1,0:T(8,128)(2,1)S(1)}, s16[1584,128]{1,0:T(8,128)(2,1)S(1)}, u32[]{:S(2)}, u32[]{:S(2)}) %collective-permute-start.25) | collective-permute-done | bytes 405536 | tf_op jit(solution)/shard_map/ppermute | solution.py:37
  191.3 2.2 %collective-permute-start.35 = (f32[24,32,128]{2,1,0:T(8,128)S(1)}, f32[24,32,128]{2,1,0:T(8,128)S(1)}, u32[]{:S(2)}, u32[]{:S(2)}) collective-permute-start(f32[24,32,128]{2,1,0:T(8,128)S(1)} %get-tuple-element.60), channel_id=1, source_target_pairs={{0,1},{1,0},{2,3},{3,2},{4,5},{5,4},{6,7},{7,6},{8,9},{9,8},{10,11... | collective-permute-start | bytes 1179656 | tf_op jit(solution)/shard_map/ppermute | solution.py:41
  (88 shorter events, 42.0 us)
Async XLA Ops:
  5.9 24.4 %collective-permute-start.9 = (bf16[4,64,2048]{2,1,0:T(8,128)(2,1)S(1)}, bf16[4,64,2048]{2,1,0:T(8,128)(2,1)S(1)}, u32[]{:S(2)}, u32[]{:S(2)}) collective-permute-start(bf16[4,64,2048]{2,1,0:T(8,128)(2,1)S(1)} %pad_maximum_fusion.refs_8_.refs_4_), channel_id=1, source_target_pairs={{0,32},{8,40},{16,48},{24,56},{32,64},{40,72},{48,80},{56,88},{64,... | collective-permute-start | bytes 3145736 | tf_op jit(solution)/shard_map/ppermute | solution.py:27
  7.2 27.1 %collective-permute-start.10 = (bf16[4,64,2048]{2,1,0:T(8,128)(2,1)S(1)}, bf16[4,64,2048]{2,1,0:T(8,128)(2,1)S(1)}, u32[]{:S(2)}, u32[]{:S(2)}) collective-permute-start(bf16[4,64,2048]{2,1,0:T(8,128)(2,1)S(1)} %pad_maximum_fusion.refs_8_.refs_4_), channel_id=1, source_target_pairs={{0,96},{8,104},{16,112},{24,120},{32,0},{40,8},{48,16},{56,24},{64... | collective-permute-start | bytes 3145736 | tf_op jit(solution)/shard_map/ppermute | solution.py:27
  7.4 86.8 %collective-permute-start.1 = (bf16[1024,1024]{1,0:T(8,128)(2,1)}, bf16[1024,1024]{1,0:T(8,128)(2,1)}, u32[]{:S(2)}, u32[]{:S(2)}) collective-permute-start(bf16[1024,1024]{1,0:T(8,128)(2,1)} %param.5), channel_id=1, source_target_pairs={{0,1},{1,0},{2,3},{3,2},{4,5},{5,4},{6,7},{7,6},{8,9},{9,8},{10,11... | collective-permute-start | bytes 6291464 | tf_op jit(solution)/shard_map/ppermute | solution.py:41
  8.4 87.8 %collective-permute-start = (bf16[1024,1024]{1,0:T(8,128)(2,1)}, bf16[1024,1024]{1,0:T(8,128)(2,1)}, u32[]{:S(2)}, u32[]{:S(2)}) collective-permute-start(bf16[1024,1024]{1,0:T(8,128)(2,1)} %param.4), channel_id=1, source_target_pairs={{0,1},{1,0},{2,3},{3,2},{4,5},{5,4},{6,7},{7,6},{8,9},{9,8},{10,11... | collective-permute-start | bytes 6291464 | tf_op jit(solution)/shard_map/ppermute | solution.py:41
  9.8 26.9 %collective-permute-start.13 = (bf16[4,64,2048]{2,1,0:T(8,128)(2,1)S(1)}, bf16[4,64,2048]{2,1,0:T(8,128)(2,1)S(1)}, u32[]{:S(2)}, u32[]{:S(2)}) collective-permute-start(bf16[4,64,2048]{2,1,0:T(8,128)(2,1)S(1)} %fusion.3.refs_13_.refs_9_), channel_id=1, source_target_pairs={{0,8},{8,16},{16,24},{24,0},{32,40},{40,48},{48,56},{56,32},{64,72... | collective-permute-start | bytes 3145736 | tf_op jit(solution)/shard_map/ppermute | solution.py:32
  30.3 25.0 %collective-permute-start.14 = (bf16[4,64,2048]{2,1,0:T(8,128)(2,1)S(1)}, bf16[4,64,2048]{2,1,0:T(8,128)(2,1)S(1)}, u32[]{:S(2)}, u32[]{:S(2)}) collective-permute-start(bf16[4,64,2048]{2,1,0:T(8,128)(2,1)S(1)} %fusion.3.refs_13_.refs_9_), channel_id=1, source_target_pairs={{0,24},{8,0},{16,8},{24,16},{32,56},{40,32},{48,40},{56,48},{64,88... | collective-permute-start | bytes 3145736 | tf_op jit(solution)/shard_map/ppermute | solution.py:32
  34.3 33.0 %collective-permute-start.11 = (bf16[2,64,2048]{2,1,0:T(8,128)(2,1)S(1)}, bf16[2,64,2048]{2,1,0:T(8,128)(2,1)S(1)}, u32[]{:S(2)}, u32[]{:S(2)}) collective-permute-start(bf16[2,64,2048]{2,1,0:T(8,128)(2,1)S(1)} %slice.44), channel_id=1, source_target_pairs={{0,32},{8,40},{16,48},{24,56},{32,64},{40,72},{48,80},{56,88},{64,... | collective-permute-start | bytes 1572872 | tf_op jit(solution)/shard_map/ppermute | solution.py:27
  36.7 20.8 %collective-permute-start.2 = (s32[16]{0:T(128)S(1)}, s32[16]{0:T(128)S(1)}, u32[]{:S(2)}, u32[]{:S(2)}) collective-permute-start(s32[16]{0:T(128)S(1)} %select_reduce_fusion.4.refs_0_.refs_4_), channel_id=1, source_target_pairs={{0,24},{8,0},{16,8},{24,16},{32,56},{40,32},{48,40},{56,48},{64,88... | collective-permute-start | bytes 200 | tf_op jit(solution)/shard_map/ppermute | solution.py:32
  90.7 15.2 %collective-permute-start.26 = (bf16[4,32,2048]{2,1,0:T(8,128)(2,1)S(1)}, bf16[4,32,2048]{2,1,0:T(8,128)(2,1)S(1)}, u32[]{:S(2)}, u32[]{:S(2)}) collective-permute-start(bf16[4,32,2048]{2,1,0:T(8,128)(2,1)S(1)} %get-tuple-element.46), channel_id=1, source_target_pairs={{0,8},{8,16},{16,24},{24,0},{32,40},{40,48},{48,56},{56,32},{64,72... | collective-permute-start | bytes 1572872 | tf_op jit(solution)/shard_map/ppermute | solution.py:32
  92.3 25.3 %collective-permute-start.27 = (bf16[4,32,2048]{2,1,0:T(8,128)(2,1)S(1)}, bf16[4,32,2048]{2,1,0:T(8,128)(2,1)S(1)}, u32[]{:S(2)}, u32[]{:S(2)}) collective-permute-start(bf16[4,32,2048]{2,1,0:T(8,128)(2,1)S(1)} %get-tuple-element.47), channel_id=1, source_target_pairs={{0,16},{8,24},{16,0},{24,8},{32,48},{40,56},{48,32},{56,40},{64,80... | collective-permute-start | bytes 1572872 | tf_op jit(solution)/shard_map/ppermute | solution.py:32
  94.2 24.5 %collective-permute-start.28 = (bf16[4,32,2048]{2,1,0:T(8,128)(2,1)S(1)}, bf16[4,32,2048]{2,1,0:T(8,128)(2,1)S(1)}, u32[]{:S(2)}, u32[]{:S(2)}) collective-permute-start(bf16[4,32,2048]{2,1,0:T(8,128)(2,1)S(1)} %get-tuple-element.48), channel_id=1, source_target_pairs={{0,24},{8,0},{16,8},{24,16},{32,56},{40,32},{48,40},{56,48},{64,88... | collective-permute-start | bytes 1572872 | tf_op jit(solution)/shard_map/ppermute | solution.py:32
  96.1 26.1 %collective-permute-start.29 = (bf16[4,32,2048]{2,1,0:T(8,128)(2,1)S(1)}, bf16[4,32,2048]{2,1,0:T(8,128)(2,1)S(1)}, u32[]{:S(2)}, u32[]{:S(2)}) collective-permute-start(bf16[4,32,2048]{2,1,0:T(8,128)(2,1)S(1)} %get-tuple-element.50), channel_id=1, source_target_pairs={{0,32},{8,40},{16,48},{24,56},{32,64},{40,72},{48,80},{56,88},{64,... | collective-permute-start | bytes 1572872 | tf_op jit(solution)/shard_map/ppermute | solution.py:27
  96.4 26.0 %collective-permute-start.30 = (bf16[4,32,2048]{2,1,0:T(8,128)(2,1)S(1)}, bf16[4,32,2048]{2,1,0:T(8,128)(2,1)S(1)}, u32[]{:S(2)}, u32[]{:S(2)}) collective-permute-start(bf16[4,32,2048]{2,1,0:T(8,128)(2,1)S(1)} %get-tuple-element.51), channel_id=1, source_target_pairs={{0,64},{8,72},{16,80},{24,88},{32,96},{40,104},{48,112},{56,120},{... | collective-permute-start | bytes 1572872 | tf_op jit(solution)/shard_map/ppermute | solution.py:27
  105.9 18.3 %collective-permute-start.31 = (bf16[4,32,2048]{2,1,0:T(8,128)(2,1)S(1)}, bf16[4,32,2048]{2,1,0:T(8,128)(2,1)S(1)}, u32[]{:S(2)}, u32[]{:S(2)}) collective-permute-start(bf16[4,32,2048]{2,1,0:T(8,128)(2,1)S(1)} %get-tuple-element.52), channel_id=1, source_target_pairs={{0,96},{8,104},{16,112},{24,120},{32,0},{40,8},{48,16},{56,24},{64... | collective-permute-start | bytes 1572872 | tf_op jit(solution)/shard_map/ppermute | solution.py:27
  117.6 19.6 %collective-permute-start.18 = (bf16[4,32,2048]{2,1,0:T(8,128)(2,1)S(1)}, bf16[4,32,2048]{2,1,0:T(8,128)(2,1)S(1)}, u32[]{:S(2)}, u32[]{:S(2)}) collective-permute-start(bf16[4,32,2048]{2,1,0:T(8,128)(2,1)S(1)} %get-tuple-element.35), channel_id=1, source_target_pairs={{0,16},{8,24},{16,0},{24,8},{32,48},{40,56},{48,32},{56,40},{64,80... | collective-permute-start | bytes 1572872 | tf_op jit(solution)/shard_map/ppermute | solution.py:32
  118.7 19.8 %collective-permute-start.19 = (bf16[4,32,2048]{2,1,0:T(8,128)(2,1)S(1)}, bf16[4,32,2048]{2,1,0:T(8,128)(2,1)S(1)}, u32[]{:S(2)}, u32[]{:S(2)}) collective-permute-start(bf16[4,32,2048]{2,1,0:T(8,128)(2,1)S(1)} %get-tuple-element.36), channel_id=1, source_target_pairs={{0,24},{8,0},{16,8},{24,16},{32,56},{40,32},{48,40},{56,48},{64,88... | collective-permute-start | bytes 1572872 | tf_op jit(solution)/shard_map/ppermute | solution.py:32
  122.3 16.2 %collective-permute-start.20 = (bf16[4,32,2048]{2,1,0:T(8,128)(2,1)S(1)}, bf16[4,32,2048]{2,1,0:T(8,128)(2,1)S(1)}, u32[]{:S(2)}, u32[]{:S(2)}) collective-permute-start(bf16[4,32,2048]{2,1,0:T(8,128)(2,1)S(1)} %get-tuple-element.38), channel_id=1, source_target_pairs={{0,32},{8,40},{16,48},{24,56},{32,64},{40,72},{48,80},{56,88},{64,... | collective-permute-start | bytes 1572872 | tf_op jit(solution)/shard_map/ppermute | solution.py:27
  122.5 16.0 %collective-permute-start.21 = (bf16[4,32,2048]{2,1,0:T(8,128)(2,1)S(1)}, bf16[4,32,2048]{2,1,0:T(8,128)(2,1)S(1)}, u32[]{:S(2)}, u32[]{:S(2)}) collective-permute-start(bf16[4,32,2048]{2,1,0:T(8,128)(2,1)S(1)} %get-tuple-element.39), channel_id=1, source_target_pairs={{0,64},{8,72},{16,80},{24,88},{32,96},{40,104},{48,112},{56,120},{... | collective-permute-start | bytes 1572872 | tf_op jit(solution)/shard_map/ppermute | solution.py:27
  124.2 20.2 %collective-permute-start.22 = (bf16[4,32,2048]{2,1,0:T(8,128)(2,1)S(1)}, bf16[4,32,2048]{2,1,0:T(8,128)(2,1)S(1)}, u32[]{:S(2)}, u32[]{:S(2)}) collective-permute-start(bf16[4,32,2048]{2,1,0:T(8,128)(2,1)S(1)} %get-tuple-element.40), channel_id=1, source_target_pairs={{0,96},{8,104},{16,112},{24,120},{32,0},{40,8},{48,16},{56,24},{64... | collective-permute-start | bytes 1572872 | tf_op jit(solution)/shard_map/ppermute | solution.py:27
  137.1 19.7 %collective-permute-start.32 = (s16[1584,128]{1,0:T(8,128)(2,1)S(1)}, s16[1584,128]{1,0:T(8,128)(2,1)S(1)}, u32[]{:S(2)}, u32[]{:S(2)}) collective-permute-start(s16[1584,128]{1,0:T(8,128)(2,1)S(1)} %get-tuple-element.54), channel_id=1, source_target_pairs={{0,2},{1,3},{2,4},{3,5},{4,6},{5,7},{6,0},{7,1},{8,10},{9,11},{10,... | collective-permute-start | bytes 1216520 | tf_op jit(solution)/shard_map/ppermute | solution.py:37
  152.5 24.5 %collective-permute-start.23 = (s16[1584,128]{1,0:T(8,128)(2,1)S(1)}, s16[1584,128]{1,0:T(8,128)(2,1)S(1)}, u32[]{:S(2)}, u32[]{:S(2)}) collective-permute-start(s16[1584,128]{1,0:T(8,128)(2,1)S(1)} %get-tuple-element.42), channel_id=1, source_target_pairs={{0,2},{1,3},{2,4},{3,5},{4,6},{5,7},{6,0},{7,1},{8,10},{9,11},{10,... | collective-permute-start | bytes 1216520 | tf_op jit(solution)/shard_map/ppermute | solution.py:37
  154.7 21.7 %collective-permute-start.34 = (s16[1584,128]{1,0:T(8,128)(2,1)S(1)}, s16[1584,128]{1,0:T(8,128)(2,1)S(1)}, u32[]{:S(2)}, u32[]{:S(2)}) collective-permute-start(s16[1584,128]{1,0:T(8,128)(2,1)S(1)} %get-tuple-element.56), channel_id=1, source_target_pairs={{0,6},{1,7},{2,0},{3,1},{4,2},{5,3},{6,4},{7,5},{8,14},{9,15},{10,... | collective-permute-start | bytes 1216520 | tf_op jit(solution)/shard_map/ppermute | solution.py:37
  156.6 21.4 %collective-permute-start.24 = (s16[1584,128]{1,0:T(8,128)(2,1)S(1)}, s16[1584,128]{1,0:T(8,128)(2,1)S(1)}, u32[]{:S(2)}, u32[]{:S(2)}) collective-permute-start(s16[1584,128]{1,0:T(8,128)(2,1)S(1)} %get-tuple-element.43), channel_id=1, source_target_pairs={{0,4},{1,5},{2,6},{3,7},{4,0},{5,1},{6,2},{7,3},{8,12},{9,13},{10,... | collective-permute-start | bytes 1216520 | tf_op jit(solution)/shard_map/ppermute | solution.py:37
  156.8 33.6 %collective-permute-start.25 = (s16[1584,128]{1,0:T(8,128)(2,1)S(1)}, s16[1584,128]{1,0:T(8,128)(2,1)S(1)}, u32[]{:S(2)}, u32[]{:S(2)}) collective-permute-start(s16[1584,128]{1,0:T(8,128)(2,1)S(1)} %get-tuple-element.44), channel_id=1, source_target_pairs={{0,6},{1,7},{2,0},{3,1},{4,2},{5,3},{6,4},{7,5},{8,14},{9,15},{10,... | collective-permute-start | bytes 1216520 | tf_op jit(solution)/shard_map/ppermute | solution.py:37
  (15 other events, 109.9 us)

commit v2 on v1

--- a/solution.py
+++ b/solution.py
@@ -41,53 +41,53 @@
     return lax.ppermute(value, "col", [(c, c ^ 1) for c in range(SIDE * 2)])
 
 
-def pick_kernel(offset, *refs):
-    wants_z, wants_x = refs[0:4], refs[4:8]
-    held = (refs[8:13], refs[13:18])
-    outs = (refs[18:22], refs[22:26])
-    sems = refs[26]
+def pick_kernel(offset, wants, *refs):
+    held = (refs[0:8], refs[8:16])
+    outs = (refs[16:20], refs[20:24])
+    sems = refs[24]
     part = pl.ds(offset, outs[0][0].shape[1])
     row = lax.axis_index("row")
     x, z = row // SIDE, row % SIDE
+    owners = SIDE * SIDE
     waits = []
-    for half in range(2):
-        own, plus, minus, far_low, far_high = held[half]
-        for away in range(SIDE):
+    for away in range(1, SIDE + 1):
+        for half in range(2):
             for near in range(SIDE):
-                if away == 0 and near == 0:
+                far = away % SIDE
+                if far == 0 and near == 0:
                     continue
                 if half == 0:
-                    choice = wants_z[away][((x + SIDE - near) % SIDE) * SIDE + z]
+                    spot = ((x + SIDE - near) % SIDE) * SIDE + z
                 else:
-                    choice = wants_x[away][x * SIDE + (z + SIDE - near) % SIDE]
-                target = outs[half][away].at[near]
-                sem = sems.at[half, away, near]
-                if near == 2:
-                    @pl.when(choice < 2)
-                    def _():
-                        pltpu.make_async_copy(far_low.at[choice, part], target, sem).start()
-
-                    @pl.when(choice >= 2)
-                    def _():
-                        pltpu.make_async_copy(far_high.at[choice - 2, part], target, sem).start()
-                else:
-                    origin = {0: own, 1: plus, 3: minus}[near]
-                    pltpu.make_async_copy(origin.at[choice, part], target, sem).start()
-                waits.append(pltpu.make_async_copy(own.at[0, part], target, sem))
+                    spot = x * SIDE + (z + SIDE - near) % SIDE
+                choice = wants[(far + (half * (SIDE - 1) if far else 0)) * owners + spot]
+                low, high = held[half][2 * near : 2 * near + 2]
+                target = outs[half][far].at[near]
+                sem = sems.at[half, far, near]
+
+                @pl.when(choice < 2)
+                def _():
+                    pltpu.make_async_copy(low.at[choice, part], target, sem).start()
+
+                @pl.when(choice >= 2)
+                def _():
+                    pltpu.make_async_copy(high.at[choice - 2, part], target, sem).start()
+
+                waits.append(pltpu.make_async_copy(low.at[0, part], target, sem))
     for copy in waits:
         copy.wait()
 
 
-def pick(wants_z, wants_x, held_a, held_b, offset, rows):
+def pick(wants, held_a, held_b, offset, rows):
     piece = jax.ShapeDtypeStruct((SIDE, rows, held_a[0].shape[2]), held_a[0].dtype)
     outs = pl.pallas_call(
         functools.partial(pick_kernel, offset),
         out_shape=[piece] * 8,
-        in_specs=[SMEM] * 8 + [ANY] * 10,
-        out_specs=[VMEM] * 8,
+        in_specs=[SMEM] + [ANY] * 16,
+        out_specs=[ANY] * 8,
         scratch_shapes=[pltpu.SemaphoreType.DMA((2, SIDE, SIDE))],
         compiler_params=pltpu.CompilerParams(vmem_limit_bytes=16 << 20),
-    )(*wants_z, *wants_x, *held_a, *held_b)
+    )(wants, *held_a, *held_b)
     return outs[:4], outs[4:]
 
 
@@ -102,9 +102,9 @@
 
 
 def product_kernel(offset, rows, slots, lists, left, *refs):
-    tables = (refs[0:5], refs[5:10])
-    kept, coded = refs[10], refs[11:14]
-    held_a, held_b, acc, sems, out_sem = refs[14:]
+    tables = (refs[0:6], refs[6:12])
+    kept, coded = refs[12], refs[13:16]
+    held_a, held_b, acc, sems, out_sem = refs[16:]
     y = lax.axis_index("col") // 2
     width = 2 * rows
     group = TILE // width
@@ -112,13 +112,14 @@
     places = slots * group
     copies = []
     for half, held in enumerate((held_a, held_b)):
-        for place in range(5):
+        for place in range(6):
             source = tables[half][place]
-            if place == 4:
+            if place < SIDE:
+                target = held.at[pl.ds(place * SIDE, SIDE)]
+            else:
                 source = source.at[:, pl.ds(offset, rows)]
-            copies.append(
-                pltpu.make_async_copy(source, held.at[pl.ds(place * SIDE, SIDE)], sems.at[half, place])
-            )
+                target = held.at[pl.ds(8 + 2 * place, 2)]
+            copies.append(pltpu.make_async_copy(source, target, sems.at[half, place]))
     for copy in copies:
         copy.start()
     for copy in copies:
@@ -184,13 +185,13 @@
     return pl.pallas_call(
         functools.partial(product_kernel, offset, rows, slots),
         out_shape=[jax.ShapeDtypeStruct((blocks, ROWS, LANES), jnp.float32)] + [code] * 3,
-        in_specs=[SMEM] + [LEFT] + [ANY] * 10,
+        in_specs=[SMEM] + [LEFT] + [ANY] * 12,
         out_specs=[ANY] + [VMEM] * 3,
         scratch_shapes=[
             pltpu.VMEM((20, rows, features), jnp.bfloat16),
             pltpu.VMEM((20, rows, features), jnp.bfloat16),
             pltpu.VMEM((SIDE, blocks + 2, ROWS, LANES), jnp.float32),
-            pltpu.SemaphoreType.DMA((2, 5)),
+            pltpu.SemaphoreType.DMA((2, 6)),
             pltpu.SemaphoreType.DMA,
         ],
         compiler_params=pltpu.CompilerParams(vmem_limit_bytes=28 << 20),
@@ -237,12 +238,14 @@
     )(kept, *coded, *earlier)
 
 
-def gather_ring(own, shift):
-    plus = shift(own, 1)
-    minus = shift(own, SIDE - 1)
-    far_low = shift(plus[:2], 1)
-    far_high = shift(minus[2:], SIDE - 1)
-    return own, plus, minus, far_low, far_high
+def gather_ring(low, high, shift):
+    plus_low = shift(low, 1)
+    minus_high = shift(high, SIDE - 1)
+    plus_high = shift(high, 1)
+    minus_low = shift(low, SIDE - 1)
+    far_low = shift(plus_low, 1)
+    far_high = shift(minus_high, SIDE - 1)
+    return [low, high, plus_low, plus_high, far_low, far_high, minus_low, minus_high]
 
 
 def shards(primal_rows, dual_rows, weight_rows, pairs):
@@ -259,10 +262,14 @@
     gotten = swap_cores(given)
     owned = lax.dynamic_slice_in_dim(weight, core * columns, columns, 1)
     owned = jnp.concatenate([owned, gotten], axis=2)
-    half_a = [owned[:, s : s + w // 2] for s, w in zip(starts, WIDTHS)]
-    half_b = [owned[:, s + w // 2 : s + w] for s, w in zip(starts, WIDTHS)]
-    held_a = gather_ring(jnp.concatenate(half_a, axis=1), shift_x)
-    held_b = gather_ring(jnp.concatenate(half_b, axis=1), shift_z)
+
+    def part(side, chosen):
+        rows = [(s + side * w // 2, s + (side + 1) * w // 2) for s, w in zip(starts, WIDTHS)]
+        return jnp.concatenate([owned[chosen, lo:hi] for lo, hi in rows], axis=1)
+
+    low, high = slice(0, 2), slice(2, 4)
+    held_a = gather_ring(part(0, low), part(0, high), shift_x)
+    held_b = gather_ring(part(1, low), part(1, high), shift_z)
     own = [v.reshape(blocks, TILE, features) for v in (primal_rows, dual_rows)]
     other = [swap_cores(v) for v in (primal_rows, dual_rows)]
     other = [v.reshape(blocks, TILE, features) for v in other]
@@ -272,8 +279,9 @@
     owner, local = second // blocks, second % blocks
     hit = owner[:, None] == jnp.arange(SIDE * SIDE, dtype=jnp.int32)[None, :]
     want = jnp.max(jnp.where(hit, local[:, None], 0), axis=0)
-    wants_z = [want] + [shift_z(want, SIDE - d) for d in range(1, SIDE)]
-    wants_x = [want] + [shift_x(want, SIDE - d) for d in range(1, SIDE)]
+    asked = [shift_z(want, SIDE - d) for d in range(1, SIDE)]
+    asked += [shift_x(want, SIDE - d) for d in range(1, SIDE)]
+    wants = jnp.concatenate([want] + asked)
     dx = (x + SIDE - owner // SIDE) % SIDE
     dz = (z + SIDE - owner % SIDE) % SIDE
     spot_a = jnp.where(owner == row, 16 + local, dz * SIDE + dx)
@@ -282,9 +290,13 @@
 
     arrived = []
     for start, width in zip(starts, WIDTHS):
-        send_a, send_b = pick(wants_z, wants_x, held_a, held_b, start // 2, width // 2)
-        table_a = [send_a[0]] + [shift_z(send_a[d], d) for d in range(1, SIDE)] + [held_a[0]]
-        table_b = [send_b[0]] + [shift_x(send_b[d], d) for d in range(1, SIDE)] + [held_b[0]]
+        send_a, send_b = pick(wants, held_a, held_b, start // 2, width // 2)
+        table_a, table_b = [send_a[0]], [send_b[0]]
+        for d in range(1, SIDE):
+            table_a.append(shift_z(send_a[d], d))
+            table_b.append(shift_x(send_b[d], d))
+        table_a += held_a[:2]
+        table_b += held_b[:2]
         arrived.append((table_a, table_b))
     outs = []
     for (table_a, table_b), start, width in zip(arrived, starts, WIDTHS):

time: 196 us -> 207 us (1.056)
  the two profiles are of different devices: /device:TPU:11 before, /device:TPU:1 now
where the time goes in v2:
time: 207 us; the launch traced here: 205 us
  waiting for transfers between devices  106 us (51%)
  starting transfers between devices  57.3 us (28%)
  Pallas kernels  28.4 us (14%)
  local copies, waits for them, and re-layouts  7.44 us (4%)
  other arithmetic  6.58 us (3%)
    ppermute x15, waiting for transfers between devices, shift_z(): return lax.ppermute(value, 'row', perm)  45.7 us
    ppermute x15, waiting for transfers between devices, shift_x(): return lax.ppermute(value, 'row', perm)  29.8 us
    ppermute x6, waiting for transfers between devices, shift_y(): return lax.ppermute(value, 'col', perm)  28.7 us
    ppermute x15, starting transfers between devices, shift_z(): return lax.ppermute(value, 'row', perm)  22.3 us
    ppermute x15, starting transfers between devices, shift_x(): return lax.ppermute(value, 'row', perm)  19.2 us
    pallas_call x2, Pallas kernels, products(): pl.pallas_call(functools.partial(product_kernel, offset, rows, slots), ou...  16.2 us
    pallas_call x2, Pallas kernels, pick(): pl.pallas_call(functools.partial(pick_kernel, offset), out_shape=[piece]...  10.6 us
    ppermute x6, starting transfers between devices, shift_y(): return lax.ppermute(value, 'col', perm)  9.21 us
  transfers between devices with their start and end apart: 40, of which 19 were waited for; matrix products, arithmetic and copies ran while one was open for 3% of the time, Pallas kernels for 13%

profile of v2, /device:TPU:1, one launch (start us, length us, event | category | flops | bytes accessed | tf_op | source)
XLA Modules:
  0.0 205.4 jit_solution(17040230764763658606)
XLA Ops:
  3.3 3.9 %collective-permute-start.2 = (s32[16]{0:T(128)S(1)}, s32[16]{0:T(128)S(1)}, u32[]{:S(2)}, u32[]{:S(2)}) collective-permute-start(s32[16]{0:T(128)S(1)} %select_reduce_fusion.4), channel_id=1, source_target_pairs={{0,24},{8,0},{16,8},{24,16},{32,56},{40,32},{48,40},{56,48},{64,88... | collective-permute-start | bytes 200 | tf_op jit(solution)/shard_map/ppermute | solution.py:32
  16.6 6.1 %collective-permute-done.5 = s32[16]{0:T(128)S(1)} collective-permute-done((s32[16]{0:T(128)S(1)}, s32[16]{0:T(128)S(1)}, u32[]{:S(2)}, u32[]{:S(2)}) %collective-permute-start.5) | collective-permute-done | bytes 96 | tf_op jit(solution)/shard_map/ppermute | solution.py:27
  23.6 10.2 %collective-permute-done.6 = s32[16]{0:T(128)S(1)} collective-permute-done((s32[16]{0:T(128)S(1)}, s32[16]{0:T(128)S(1)}, u32[]{:S(2)}, u32[]{:S(2)}) %collective-permute-start.6) | collective-permute-done | bytes 96 | tf_op jit(solution)/shard_map/ppermute | solution.py:27
  39.4 6.6 %collective-permute-done.14.refs_6_ = bf16[2,64,2048]{2,1,0:T(8,128)(2,1)} collective-permute-done((bf16[2,64,2048]{2,1,0:T(8,128)(2,1)S(1)}, bf16[2,64,2048]{2,1,0:T(8,128)(2,1)}, u32[]{:S(2)}, u32[]{:S(2)}) %collective-permute-start.14) | collective-permute-done | bytes 524320 | tf_op jit(solution)/shard_map/ppermute | solution.py:27
  48.7 9.8 %collective-permute-done.16.refs_11_ = bf16[2,64,2048]{2,1,0:T(8,128)(2,1)} collective-permute-done((bf16[2,64,2048]{2,1,0:T(8,128)(2,1)S(1)}, bf16[2,64,2048]{2,1,0:T(8,128)(2,1)}, u32[]{:S(2)}, u32[]{:S(2)}) %collective-permute-start.16) | collective-permute-done | bytes 524320 | tf_op jit(solution)/shard_map/ppermute | solution.py:32
  61.3 7.1 %collective-permute-done.20.refs_14_ = bf16[2,64,2048]{2,1,0:T(8,128)(2,1)S(1)} collective-permute-done((bf16[2,64,2048]{2,1,0:T(8,128)(2,1)S(1)}, bf16[2,64,2048]{2,1,0:T(8,128)(2,1)S(1)}, u32[]{:S(2)}, u32[]{:S(2)}) %collective-permute-start.20) | collective-permute-done | bytes 524320 | tf_op jit(solution)/shard_map/ppermute | solution.py:32
  73.6 8.1 %collective-permute-done.17.refs_12_ = bf16[2,64,2048]{2,1,0:T(8,128)(2,1)} collective-permute-done((bf16[2,64,2048]{2,1,0:T(8,128)(2,1)}, bf16[2,64,2048]{2,1,0:T(8,128)(2,1)}, u32[]{:S(2)}, u32[]{:S(2)}) %collective-permute-start.17) | collective-permute-done | bytes 524320 | tf_op jit(solution)/shard_map/ppermute | solution.py:32
  85.3 5.3 %shard_map.46 = (bf16[4,32,2048]{2,1,0:T(8,128)(2,1)S(1)}, bf16[4,32,2048]{2,1,0:T(8,128)(2,1)S(1)}, bf16[4,32,2048]{2,1,0:T(8,128)(2,1)S(1)}, bf16[4,32,2048]{2...) custom-call(s32[112]{0:T(128)S(1)} %concatenate.38.wants, ...), custom_call_target="tpu_custom_call" | custom-call | tf_op jit(solution)/shard_map/pallas_call | solution.py:83
  91.6 5.3 %shard_map.48 = (bf16[4,32,2048]{2,1,0:T(8,128)(2,1)S(1)}, bf16[4,32,2048]{2,1,0:T(8,128)(2,1)S(1)}, bf16[4,32,2048]{2,1,0:T(8,128)(2,1)S(1)}, bf16[4,32,2048]{2...) custom-call(s32[112]{0:T(128)S(1)} %concatenate.38.wants, ...), custom_call_target="tpu_custom_call" | custom-call | tf_op jit(solution)/shard_map/pallas_call | solution.py:83
  102.6 2.6 %collective-permute-start.34 = (bf16[4,32,2048]{2,1,0:T(8,128)(2,1)S(1)}, bf16[4,32,2048]{2,1,0:T(8,128)(2,1)S(1)}, u32[]{:S(2)}, u32[]{:S(2)}) collective-permute-start(bf16[4,32,2048]{2,1,0:T(8,128)(2,1)S(1)} %get-tuple-element.51), channel_id=1, source_target_pairs={{0,64},{8,72},{16,80},{24,88},{32,96},{40,104},{48,112},{56,120},{... | collective-permute-start | bytes 1572872 | tf_op jit(solution)/shard_map/ppermute | solution.py:27
  105.3 7.4 %collective-permute-done.30.refs_1_ = bf16[4,32,2048]{2,1,0:T(8,128)(2,1)S(1)} collective-permute-done((bf16[4,32,2048]{2,1,0:T(8,128)(2,1)S(1)}, bf16[4,32,2048]{2,1,0:T(8,128)(2,1)S(1)}, u32[]{:S(2)}, u32[]{:S(2)}) %collective-permute-start.30) | collective-permute-done | bytes 524320 | tf_op jit(solution)/shard_map/ppermute | solution.py:32
  115.3 9.8 %collective-permute-done.31.refs_2_ = bf16[4,32,2048]{2,1,0:T(8,128)(2,1)S(1)} collective-permute-done((bf16[4,32,2048]{2,1,0:T(8,128)(2,1)S(1)}, bf16[4,32,2048]{2,1,0:T(8,128)(2,1)S(1)}, u32[]{:S(2)}, u32[]{:S(2)}) %collective-permute-start.31) | collective-permute-done | bytes 524320 | tf_op jit(solution)/shard_map/ppermute | solution.py:32
  126.1 3.9 %collective-permute-start.23 = (bf16[4,32,2048]{2,1,0:T(8,128)(2,1)S(1)}, bf16[4,32,2048]{2,1,0:T(8,128)(2,1)S(1)}, u32[]{:S(2)}, u32[]{:S(2)}) collective-permute-start(bf16[4,32,2048]{2,1,0:T(8,128)(2,1)S(1)} %get-tuple-element.36), channel_id=1, source_target_pairs={{0,24},{8,0},{16,8},{24,16},{32,56},{40,32},{48,40},{56,48},{64,88... | collective-permute-start | bytes 1572872 | tf_op jit(solution)/shard_map/ppermute | solution.py:32
  130.0 3.6 %collective-permute-start.25 = (bf16[4,32,2048]{2,1,0:T(8,128)(2,1)S(1)}, bf16[4,32,2048]{2,1,0:T(8,128)(2,1)S(1)}, u32[]{:S(2)}, u32[]{:S(2)}) collective-permute-start(bf16[4,32,2048]{2,1,0:T(8,128)(2,1)S(1)} %get-tuple-element.39), channel_id=1, source_target_pairs={{0,64},{8,72},{16,80},{24,88},{32,96},{40,104},{48,112},{56,120},{... | collective-permute-start | bytes 1572872 | tf_op jit(solution)/shard_map/ppermute | solution.py:27
  134.2 4.3 %maximum_maximum_fusion.left = bf16[4,512,2048]{2,1,0:T(8,128)(2,1)S(1)} fusion(bf16[4,256,1024]{2,1,0:T(8,128)(2,1)} %bitcast.6, bf16[4,256,1024]{2,1,0:T(8,128)(2,1)} %bitcast.5, bf16[4,256,1024]{2,1,0:T(8,128)(2,1)} %bitcast.4, bf16[4,256,1024]{2,1,0:T(8,128)(2,1)} %bitcast.3), kind=kLoop, calls=%fused_computation | loop fusion | flops 33554432 | bytes 16777216 | tf_op jit(solution)/shard_map/concatenate | solution.py:276
  138.5 8.1 %shard_map.49 = (f32[48,32,128]{2,1,0:T(8,128)S(1)}, s16[1584,128]{1,0:T(8,128)(2,1)S(1)}, s16[1584,128]{1,0:T(8,128)(2,1)S(1)}, s16[1584,128]{1,0:T(8,128)(2,1)S(1)}) custom-call(s32[117]{0:T(128)S(1)} %pad_add_fusion.lists, bf16[4,512,2048]{2,1,0:T(8,128)(2,1)S(1)} %maximum_maximum_fusion.left, bf16[4,32,2048]{2,1,0:T(8,128)(2,1)S(1)} %get-tuple-element.45.refs_0_, ...), custom_call_target="tpu_custom_call" | custom-call | tf_op jit(solution)/shard_map/pallas_call | solution.py:185
  148.0 5.1 %collective-permute-done.25.refs_8_ = bf16[4,32,2048]{2,1,0:T(8,128)(2,1)S(1)} collective-permute-done((bf16[4,32,2048]{2,1,0:T(8,128)(2,1)S(1)}, bf16[4,32,2048]{2,1,0:T(8,128)(2,1)S(1)}, u32[]{:S(2)}, u32[]{:S(2)}) %collective-permute-start.25) | collective-permute-done | bytes 524320 | tf_op jit(solution)/shard_map/ppermute | solution.py:27
  154.0 8.1 %shard_map.47 = (f32[48,32,128]{2,1,0:T(8,128)S(1)}, s16[1584,128]{1,0:T(8,128)(2,1)S(1)}, s16[1584,128]{1,0:T(8,128)(2,1)S(1)}, s16[1584,128]{1,0:T(8,128)(2,1)S(1)}) custom-call(s32[117]{0:T(128)S(1)} %pad_add_fusion.lists, bf16[4,512,2048]{2,1,0:T(8,128)(2,1)S(1)} %maximum_maximum_fusion.left, bf16[4,32,2048]{2,1,0:T(8,128)(2,1)S(1)} %get-tuple-element.33.refs_0_, ...), custom_call_target="tpu_custom_call" | custom-call | tf_op jit(solution)/shard_map/pallas_call | solution.py:185
  163.4 2.6 %collective-permute-start.37 = (s16[1584,128]{1,0:T(8,128)(2,1)S(1)}, s16[1584,128]{1,0:T(8,128)(2,1)S(1)}, u32[]{:S(2)}, u32[]{:S(2)}) collective-permute-start(s16[1584,128]{1,0:T(8,128)(2,1)S(1)} %get-tuple-element.55), channel_id=1, source_target_pairs={{0,4},{1,5},{2,6},{3,7},{4,0},{5,1},{6,2},{7,3},{8,12},{9,13},{10,... | collective-permute-start | bytes 1216520 | tf_op jit(solution)/shard_map/ppermute | solution.py:37
  169.9 10.4 %collective-permute-done.37.refs_1_ = s16[1584,128]{1,0:T(8,128)(2,1)S(1)} collective-permute-done((s16[1584,128]{1,0:T(8,128)(2,1)S(1)}, s16[1584,128]{1,0:T(8,128)(2,1)S(1)}, u32[]{:S(2)}, u32[]{:S(2)}) %collective-permute-start.37) | collective-permute-done | bytes 405536 | tf_op jit(solution)/shard_map/ppermute | solution.py:37
  180.4 4.2 %collective-permute-done.38.refs_2_ = s16[1584,128]{1,0:T(8,128)(2,1)S(1)} collective-permute-done((s16[1584,128]{1,0:T(8,128)(2,1)S(1)}, s16[1584,128]{1,0:T(8,128)(2,1)S(1)}, u32[]{:S(2)}, u32[]{:S(2)}) %collective-permute-start.38) | collective-permute-done | bytes 405536 | tf_op jit(solution)/shard_map/ppermute | solution.py:37
  185.1 3.9 %collective-permute-done.28.refs_1_ = s16[1584,128]{1,0:T(8,128)(2,1)S(1)} collective-permute-done((s16[1584,128]{1,0:T(8,128)(2,1)S(1)}, s16[1584,128]{1,0:T(8,128)(2,1)S(1)}, u32[]{:S(2)}, u32[]{:S(2)}) %collective-permute-start.28) | collective-permute-done | bytes 405536 | tf_op jit(solution)/shard_map/ppermute | solution.py:37
  189.0 10.2 %collective-permute-done.29.refs_2_ = s16[1584,128]{1,0:T(8,128)(2,1)S(1)} collective-permute-done((s16[1584,128]{1,0:T(8,128)(2,1)S(1)}, s16[1584,128]{1,0:T(8,128)(2,1)S(1)}, u32[]{:S(2)}, u32[]{:S(2)}) %collective-permute-start.29) | collective-permute-done | bytes 405536 | tf_op jit(solution)/shard_map/ppermute | solution.py:37
  200.2 2.8 %collective-permute-start.39 = (f32[24,32,128]{2,1,0:T(8,128)S(1)}, f32[24,32,128]{2,1,0:T(8,128)S(1)}, u32[]{:S(2)}, u32[]{:S(2)}) collective-permute-start(f32[24,32,128]{2,1,0:T(8,128)S(1)} %get-tuple-element.60), channel_id=1, source_target_pairs={{0,1},{1,0},{2,3},{3,2},{4,5},{5,4},{6,7},{7,6},{8,9},{9,8},{10,11... | collective-permute-start | bytes 1179656 | tf_op jit(solution)/shard_map/ppermute | solution.py:41
  (103 shorter events, 55.7 us)
Async XLA Ops:
  7.5 26.8 %collective-permute-start.9 = (bf16[2,64,2048]{2,1,0:T(8,128)(2,1)S(1)}, bf16[2,64,2048]{2,1,0:T(8,128)(2,1)S(1)}, u32[]{:S(2)}, u32[]{:S(2)}) collective-permute-start(bf16[2,64,2048]{2,1,0:T(8,128)(2,1)S(1)} %pad_maximum_fusion.1.refs_0_.refs_4_), channel_id=1, source_target_pairs={{0,32},{8,40},{16,48},{24,56},{32,64},{40,72},{48,80},{56,88},{64,... | collective-permute-start | bytes 1572872 | tf_op jit(solution)/shard_map/ppermute | solution.py:27
  8.8 27.4 %collective-permute-start.10 = (bf16[2,64,2048]{2,1,0:T(8,128)(2,1)S(1)}, bf16[2,64,2048]{2,1,0:T(8,128)(2,1)S(1)}, u32[]{:S(2)}, u32[]{:S(2)}) collective-permute-start(bf16[2,64,2048]{2,1,0:T(8,128)(2,1)S(1)} %pad_maximum_fusion.2.refs_1_.refs_5_), channel_id=1, source_target_pairs={{0,32},{8,40},{16,48},{24,56},{32,64},{40,72},{48,80},{56,88},{64,... | collective-permute-start | bytes 1572872 | tf_op jit(solution)/shard_map/ppermute | solution.py:27
  10.1 28.5 %collective-permute-start.12 = (bf16[2,64,2048]{2,1,0:T(8,128)(2,1)S(1)}, bf16[2,64,2048]{2,1,0:T(8,128)(2,1)S(1)}, u32[]{:S(2)}, u32[]{:S(2)}) collective-permute-start(bf16[2,64,2048]{2,1,0:T(8,128)(2,1)S(1)} %pad_maximum_fusion.2.refs_1_.refs_5_), channel_id=1, source_target_pairs={{0,96},{8,104},{16,112},{24,120},{32,0},{40,8},{48,16},{56,24},{64... | collective-permute-start | bytes 1572872 | tf_op jit(solution)/shard_map/ppermute | solution.py:27
  15.6 18.2 %collective-permute-start.6 = (s32[16]{0:T(128)S(1)}, s32[16]{0:T(128)S(1)}, u32[]{:S(2)}, u32[]{:S(2)}) collective-permute-start(s32[16]{0:T(128)S(1)} %select_reduce_fusion.4), channel_id=1, source_target_pairs={{0,64},{8,72},{16,80},{24,88},{32,96},{40,104},{48,112},{56,120},{... | collective-permute-start | bytes 200 | tf_op jit(solution)/shard_map/ppermute | solution.py:27
  34.3 24.1 %collective-permute-start.16 = (bf16[2,64,2048]{2,1,0:T(8,128)(2,1)S(1)}, bf16[2,64,2048]{2,1,0:T(8,128)(2,1)}, u32[]{:S(2)}, u32[]{:S(2)}) collective-permute-start(bf16[2,64,2048]{2,1,0:T(8,128)(2,1)S(1)} %fusion.3.refs_9_.refs_11_), channel_id=1, source_target_pairs={{0,8},{8,16},{16,24},{24,0},{32,40},{40,48},{48,56},{56,32},{64,72... | collective-permute-start | bytes 1572872 | tf_op jit(solution)/shard_map/ppermute | solution.py:32
  36.2 64.3 %collective-permute-start.1 = (bf16[1024,1024]{1,0:T(8,128)(2,1)}, bf16[1024,1024]{1,0:T(8,128)(2,1)}, u32[]{:S(2)}, u32[]{:S(2)}) collective-permute-start(bf16[1024,1024]{1,0:T(8,128)(2,1)} %param.5), channel_id=1, source_target_pairs={{0,1},{1,0},{2,3},{3,2},{4,5},{5,4},{6,7},{7,6},{8,9},{9,8},{10,11... | collective-permute-start | bytes 6291464 | tf_op jit(solution)/shard_map/ppermute | solution.py:41
  39.4 63.3 %collective-permute-start = (bf16[1024,1024]{1,0:T(8,128)(2,1)}, bf16[1024,1024]{1,0:T(8,128)(2,1)}, u32[]{:S(2)}, u32[]{:S(2)}) collective-permute-start(bf16[1024,1024]{1,0:T(8,128)(2,1)} %param.4), channel_id=1, source_target_pairs={{0,1},{1,0},{2,3},{3,2},{4,5},{5,4},{6,7},{7,6},{8,9},{9,8},{10,11... | collective-permute-start | bytes 6291464 | tf_op jit(solution)/shard_map/ppermute | solution.py:41
  47.9 20.6 %collective-permute-start.20 = (bf16[2,64,2048]{2,1,0:T(8,128)(2,1)S(1)}, bf16[2,64,2048]{2,1,0:T(8,128)(2,1)S(1)}, u32[]{:S(2)}, u32[]{:S(2)}) collective-permute-start(bf16[2,64,2048]{2,1,0:T(8,128)(2,1)S(1)} %pad_maximum_fusion.3.refs_8_.refs_10_), channel_id=1, source_target_pairs={{0,24},{8,0},{16,8},{24,16},{32,56},{40,32},{48,40},{56,48},{64,88... | collective-permute-start | bytes 1572872 | tf_op jit(solution)/shard_map/ppermute | solution.py:32
  98.6 26.4 %collective-permute-start.31 = (bf16[4,32,2048]{2,1,0:T(8,128)(2,1)S(1)}, bf16[4,32,2048]{2,1,0:T(8,128)(2,1)S(1)}, u32[]{:S(2)}, u32[]{:S(2)}) collective-permute-start(bf16[4,32,2048]{2,1,0:T(8,128)(2,1)S(1)} %get-tuple-element.47), channel_id=1, source_target_pairs={{0,16},{8,24},{16,0},{24,8},{32,48},{40,56},{48,32},{56,40},{64,80... | collective-permute-start | bytes 1572872 | tf_op jit(solution)/shard_map/ppermute | solution.py:32
  100.6 25.5 %collective-permute-start.32 = (bf16[4,32,2048]{2,1,0:T(8,128)(2,1)S(1)}, bf16[4,32,2048]{2,1,0:T(8,128)(2,1)S(1)}, u32[]{:S(2)}, u32[]{:S(2)}) collective-permute-start(bf16[4,32,2048]{2,1,0:T(8,128)(2,1)S(1)} %get-tuple-element.48), channel_id=1, source_target_pairs={{0,24},{8,0},{16,8},{24,16},{32,56},{40,32},{48,40},{56,48},{64,88... | collective-permute-start | bytes 1572872 | tf_op jit(solution)/shard_map/ppermute | solution.py:32
  102.6 27.4 %collective-permute-start.33 = (bf16[4,32,2048]{2,1,0:T(8,128)(2,1)S(1)}, bf16[4,32,2048]{2,1,0:T(8,128)(2,1)S(1)}, u32[]{:S(2)}, u32[]{:S(2)}) collective-permute-start(bf16[4,32,2048]{2,1,0:T(8,128)(2,1)S(1)} %get-tuple-element.50), channel_id=1, source_target_pairs={{0,32},{8,40},{16,48},{24,56},{32,64},{40,72},{48,80},{56,88},{64,... | collective-permute-start | bytes 1572872 | tf_op jit(solution)/shard_map/ppermute | solution.py:27
  102.6 27.3 %collective-permute-start.34 = (bf16[4,32,2048]{2,1,0:T(8,128)(2,1)S(1)}, bf16[4,32,2048]{2,1,0:T(8,128)(2,1)S(1)}, u32[]{:S(2)}, u32[]{:S(2)}) collective-permute-start(bf16[4,32,2048]{2,1,0:T(8,128)(2,1)S(1)} %get-tuple-element.51), channel_id=1, source_target_pairs={{0,64},{8,72},{16,80},{24,88},{32,96},{40,104},{48,112},{56,120},{... | collective-permute-start | bytes 1572872 | tf_op jit(solution)/shard_map/ppermute | solution.py:27
  112.7 20.8 %collective-permute-start.35 = (bf16[4,32,2048]{2,1,0:T(8,128)(2,1)S(1)}, bf16[4,32,2048]{2,1,0:T(8,128)(2,1)S(1)}, u32[]{:S(2)}, u32[]{:S(2)}) collective-permute-start(bf16[4,32,2048]{2,1,0:T(8,128)(2,1)S(1)} %get-tuple-element.52), channel_id=1, source_target_pairs={{0,96},{8,104},{16,112},{24,120},{32,0},{40,8},{48,16},{56,24},{64... | collective-permute-start | bytes 1572872 | tf_op jit(solution)/shard_map/ppermute | solution.py:27
  125.0 21.6 %collective-permute-start.22 = (bf16[4,32,2048]{2,1,0:T(8,128)(2,1)S(1)}, bf16[4,32,2048]{2,1,0:T(8,128)(2,1)S(1)}, u32[]{:S(2)}, u32[]{:S(2)}) collective-permute-start(bf16[4,32,2048]{2,1,0:T(8,128)(2,1)S(1)} %get-tuple-element.35), channel_id=1, source_target_pairs={{0,16},{8,24},{16,0},{24,8},{32,48},{40,56},{48,32},{56,40},{64,80... | collective-permute-start | bytes 1572872 | tf_op jit(solution)/shard_map/ppermute | solution.py:32
  126.1 21.9 %collective-permute-start.23 = (bf16[4,32,2048]{2,1,0:T(8,128)(2,1)S(1)}, bf16[4,32,2048]{2,1,0:T(8,128)(2,1)S(1)}, u32[]{:S(2)}, u32[]{:S(2)}) collective-permute-start(bf16[4,32,2048]{2,1,0:T(8,128)(2,1)S(1)} %get-tuple-element.36), channel_id=1, source_target_pairs={{0,24},{8,0},{16,8},{24,16},{32,56},{40,32},{48,40},{56,48},{64,88... | collective-permute-start | bytes 1572872 | tf_op jit(solution)/shard_map/ppermute | solution.py:32
  130.0 18.0 %collective-permute-start.24 = (bf16[4,32,2048]{2,1,0:T(8,128)(2,1)S(1)}, bf16[4,32,2048]{2,1,0:T(8,128)(2,1)S(1)}, u32[]{:S(2)}, u32[]{:S(2)}) collective-permute-start(bf16[4,32,2048]{2,1,0:T(8,128)(2,1)S(1)} %get-tuple-element.38), channel_id=1, source_target_pairs={{0,32},{8,40},{16,48},{24,56},{32,64},{40,72},{48,80},{56,88},{64,... | collective-permute-start | bytes 1572872 | tf_op jit(solution)/shard_map/ppermute | solution.py:27
  130.0 23.1 %collective-permute-start.25 = (bf16[4,32,2048]{2,1,0:T(8,128)(2,1)S(1)}, bf16[4,32,2048]{2,1,0:T(8,128)(2,1)S(1)}, u32[]{:S(2)}, u32[]{:S(2)}) collective-permute-start(bf16[4,32,2048]{2,1,0:T(8,128)(2,1)S(1)} %get-tuple-element.39), channel_id=1, source_target_pairs={{0,64},{8,72},{16,80},{24,88},{32,96},{40,104},{48,112},{56,120},{... | collective-permute-start | bytes 1572872 | tf_op jit(solution)/shard_map/ppermute | solution.py:27
  133.6 20.4 %collective-permute-start.26 = (bf16[4,32,2048]{2,1,0:T(8,128)(2,1)S(1)}, bf16[4,32,2048]{2,1,0:T(8,128)(2,1)S(1)}, u32[]{:S(2)}, u32[]{:S(2)}) collective-permute-start(bf16[4,32,2048]{2,1,0:T(8,128)(2,1)S(1)} %get-tuple-element.40), channel_id=1, source_target_pairs={{0,96},{8,104},{16,112},{24,120},{32,0},{40,8},{48,16},{56,24},{64... | collective-permute-start | bytes 1572872 | tf_op jit(solution)/shard_map/ppermute | solution.py:27
  146.6 20.7 %collective-permute-start.36 = (s16[1584,128]{1,0:T(8,128)(2,1)S(1)}, s16[1584,128]{1,0:T(8,128)(2,1)S(1)}, u32[]{:S(2)}, u32[]{:S(2)}) collective-permute-start(s16[1584,128]{1,0:T(8,128)(2,1)S(1)} %get-tuple-element.54), channel_id=1, source_target_pairs={{0,2},{1,3},{2,4},{3,5},{4,6},{5,7},{6,0},{7,1},{8,10},{9,11},{10,... | collective-permute-start | bytes 1216520 | tf_op jit(solution)/shard_map/ppermute | solution.py:37
  162.1 23.0 %collective-permute-start.27 = (s16[1584,128]{1,0:T(8,128)(2,1)S(1)}, s16[1584,128]{1,0:T(8,128)(2,1)S(1)}, u32[]{:S(2)}, u32[]{:S(2)}) collective-permute-start(s16[1584,128]{1,0:T(8,128)(2,1)S(1)} %get-tuple-element.42), channel_id=1, source_target_pairs={{0,2},{1,3},{2,4},{3,5},{4,6},{5,7},{6,0},{7,1},{8,10},{9,11},{10,... | collective-permute-start | bytes 1216520 | tf_op jit(solution)/shard_map/ppermute | solution.py:37
  163.4 16.9 %collective-permute-start.37 = (s16[1584,128]{1,0:T(8,128)(2,1)S(1)}, s16[1584,128]{1,0:T(8,128)(2,1)S(1)}, u32[]{:S(2)}, u32[]{:S(2)}) collective-permute-start(s16[1584,128]{1,0:T(8,128)(2,1)S(1)} %get-tuple-element.55), channel_id=1, source_target_pairs={{0,4},{1,5},{2,6},{3,7},{4,0},{5,1},{6,2},{7,3},{8,12},{9,13},{10,... | collective-permute-start | bytes 1216520 | tf_op jit(solution)/shard_map/ppermute | solution.py:37
  166.1 18.4 %collective-permute-start.38 = (s16[1584,128]{1,0:T(8,128)(2,1)S(1)}, s16[1584,128]{1,0:T(8,128)(2,1)S(1)}, u32[]{:S(2)}, u32[]{:S(2)}) collective-permute-start(s16[1584,128]{1,0:T(8,128)(2,1)S(1)} %get-tuple-element.56), channel_id=1, source_target_pairs={{0,6},{1,7},{2,0},{3,1},{4,2},{5,3},{6,4},{7,5},{8,14},{9,15},{10,... | collective-permute-start | bytes 1216520 | tf_op jit(solution)/shard_map/ppermute | solution.py:37
  167.1 21.9 %collective-permute-start.28 = (s16[1584,128]{1,0:T(8,128)(2,1)S(1)}, s16[1584,128]{1,0:T(8,128)(2,1)S(1)}, u32[]{:S(2)}, u32[]{:S(2)}) collective-permute-start(s16[1584,128]{1,0:T(8,128)(2,1)S(1)} %get-tuple-element.43), channel_id=1, source_target_pairs={{0,4},{1,5},{2,6},{3,7},{4,0},{5,1},{6,2},{7,3},{8,12},{9,13},{10,... | collective-permute-start | bytes 1216520 | tf_op jit(solution)/shard_map/ppermute | solution.py:37
  167.3 31.9 %collective-permute-start.29 = (s16[1584,128]{1,0:T(8,128)(2,1)S(1)}, s16[1584,128]{1,0:T(8,128)(2,1)S(1)}, u32[]{:S(2)}, u32[]{:S(2)}) collective-permute-start(s16[1584,128]{1,0:T(8,128)(2,1)S(1)} %get-tuple-element.44), channel_id=1, source_target_pairs={{0,6},{1,7},{2,0},{3,1},{4,2},{5,3},{6,4},{7,5},{8,14},{9,15},{10,... | collective-permute-start | bytes 1216520 | tf_op jit(solution)/shard_map/ppermute | solution.py:37
  (23 other events, 174.4 us)

commit v3 on v2

--- a/solution.py
+++ b/solution.py
@@ -146,7 +146,7 @@
                 acc[away, pl.ds(tile * 2, 2)] = parts[target]
         return carry
 
-    lax.fori_loop(0, slots, one, 0, unroll=3)
+    lax.fori_loop(0, slots, one, 0, unroll=9)
     keep = pltpu.make_async_copy(acc.at[0, pl.ds(0, blocks)], kept, out_sem)
     keep.start()
     for d in range(1, SIDE):
@@ -302,7 +302,9 @@
     for (table_a, table_b), start, width in zip(arrived, starts, WIDTHS):
         slots, lists = grouped(first, spot_a, spot_b, TILE // width)
         kept, *coded = products(lists, slots, left, table_a, table_b, start // 2, width // 2, tiles)
-        moved = [shift_y(code, d + 1) for d, code in enumerate(coded)]
+        moved = []
+        for d, code in enumerate(coded):
+            moved.append(shift_y(code, d + 1))
         outs = finish(kept, moved, outs)
     mine, theirs = outs
     theirs = swap_cores(theirs)

time: 207 us -> 206 us (level)
  no operation moved by 1% of the time
where the time goes in v3:
time: 206 us; the launch traced here: 205 us
  waiting for transfers between devices  106 us (51%)
  starting transfers between devices  57.5 us (28%)
  Pallas kernels  26.9 us (13%)
  local copies, waits for them, and re-layouts  7.44 us (4%)
  other arithmetic  6.58 us (3%)
    ppermute x15, waiting for transfers between devices, shift_z(): return lax.ppermute(value, 'row', perm)  45.7 us
    ppermute x15, waiting for transfers between devices, shift_x(): return lax.ppermute(value, 'row', perm)  30.3 us
    ppermute x6, waiting for transfers between devices, shift_y(): return lax.ppermute(value, 'col', perm)  28.7 us
    ppermute x15, starting transfers between devices, shift_z(): return lax.ppermute(value, 'row', perm)  22.3 us
    ppermute x15, starting transfers between devices, shift_x(): return lax.ppermute(value, 'row', perm)  19.2 us
    pallas_call x2, Pallas kernels, products(): pl.pallas_call(functools.partial(product_kernel, offset, rows, slots), ou...  14.7 us
    pallas_call x2, Pallas kernels, pick(): pl.pallas_call(functools.partial(pick_kernel, offset), out_shape=[piece]...  10.6 us
    ppermute x6, starting transfers between devices, shift_y(): return lax.ppermute(value, 'col', perm)  9.43 us
  transfers between devices with their start and end apart: 40, of which 19 were waited for; matrix products, arithmetic and copies ran while one was open for 3% of the time, Pallas kernels for 13%

profile of v3, /device:TPU:1, one launch (start us, length us, event | category | flops | bytes accessed | tf_op | source)
XLA Modules:
  0.0 204.6 jit_solution(412723489928055882)
XLA Ops:
  3.3 3.9 %collective-permute-start.2 = (s32[16]{0:T(128)S(1)}, s32[16]{0:T(128)S(1)}, u32[]{:S(2)}, u32[]{:S(2)}) collective-permute-start(s32[16]{0:T(128)S(1)} %select_reduce_fusion.4), channel_id=1, source_target_pairs={{0,24},{8,0},{16,8},{24,16},{32,56},{40,32},{48,40},{56,48},{64,88... | collective-permute-start | bytes 200 | tf_op jit(solution)/shard_map/ppermute | solution.py:32
  16.6 6.1 %collective-permute-done.5 = s32[16]{0:T(128)S(1)} collective-permute-done((s32[16]{0:T(128)S(1)}, s32[16]{0:T(128)S(1)}, u32[]{:S(2)}, u32[]{:S(2)}) %collective-permute-start.5) | collective-permute-done | bytes 96 | tf_op jit(solution)/shard_map/ppermute | solution.py:27
  23.6 10.2 %collective-permute-done.6 = s32[16]{0:T(128)S(1)} collective-permute-done((s32[16]{0:T(128)S(1)}, s32[16]{0:T(128)S(1)}, u32[]{:S(2)}, u32[]{:S(2)}) %collective-permute-start.6) | collective-permute-done | bytes 96 | tf_op jit(solution)/shard_map/ppermute | solution.py:27
  39.4 6.6 %collective-permute-done.14.refs_6_ = bf16[2,64,2048]{2,1,0:T(8,128)(2,1)} collective-permute-done((bf16[2,64,2048]{2,1,0:T(8,128)(2,1)S(1)}, bf16[2,64,2048]{2,1,0:T(8,128)(2,1)}, u32[]{:S(2)}, u32[]{:S(2)}) %collective-permute-start.14) | collective-permute-done | bytes 524320 | tf_op jit(solution)/shard_map/ppermute | solution.py:27
  48.7 9.8 %collective-permute-done.16.refs_11_ = bf16[2,64,2048]{2,1,0:T(8,128)(2,1)} collective-permute-done((bf16[2,64,2048]{2,1,0:T(8,128)(2,1)S(1)}, bf16[2,64,2048]{2,1,0:T(8,128)(2,1)}, u32[]{:S(2)}, u32[]{:S(2)}) %collective-permute-start.16) | collective-permute-done | bytes 524320 | tf_op jit(solution)/shard_map/ppermute | solution.py:32
  61.3 7.1 %collective-permute-done.20.refs_14_ = bf16[2,64,2048]{2,1,0:T(8,128)(2,1)S(1)} collective-permute-done((bf16[2,64,2048]{2,1,0:T(8,128)(2,1)S(1)}, bf16[2,64,2048]{2,1,0:T(8,128)(2,1)S(1)}, u32[]{:S(2)}, u32[]{:S(2)}) %collective-permute-start.20) | collective-permute-done | bytes 524320 | tf_op jit(solution)/shard_map/ppermute | solution.py:32
  73.6 8.1 %collective-permute-done.17.refs_12_ = bf16[2,64,2048]{2,1,0:T(8,128)(2,1)} collective-permute-done((bf16[2,64,2048]{2,1,0:T(8,128)(2,1)}, bf16[2,64,2048]{2,1,0:T(8,128)(2,1)}, u32[]{:S(2)}, u32[]{:S(2)}) %collective-permute-start.17) | collective-permute-done | bytes 524320 | tf_op jit(solution)/shard_map/ppermute | solution.py:32
  85.3 5.3 %shard_map.46 = (bf16[4,32,2048]{2,1,0:T(8,128)(2,1)S(1)}, bf16[4,32,2048]{2,1,0:T(8,128)(2,1)S(1)}, bf16[4,32,2048]{2,1,0:T(8,128)(2,1)S(1)}, bf16[4,32,2048]{2...) custom-call(s32[112]{0:T(128)S(1)} %concatenate.38.wants, ...), custom_call_target="tpu_custom_call" | custom-call | tf_op jit(solution)/shard_map/pallas_call | solution.py:83
  91.6 5.3 %shard_map.48 = (bf16[4,32,2048]{2,1,0:T(8,128)(2,1)S(1)}, bf16[4,32,2048]{2,1,0:T(8,128)(2,1)S(1)}, bf16[4,32,2048]{2,1,0:T(8,128)(2,1)S(1)}, bf16[4,32,2048]{2...) custom-call(s32[112]{0:T(128)S(1)} %concatenate.38.wants, ...), custom_call_target="tpu_custom_call" | custom-call | tf_op jit(solution)/shard_map/pallas_call | solution.py:83
  102.6 2.6 %collective-permute-start.34 = (bf16[4,32,2048]{2,1,0:T(8,128)(2,1)S(1)}, bf16[4,32,2048]{2,1,0:T(8,128)(2,1)S(1)}, u32[]{:S(2)}, u32[]{:S(2)}) collective-permute-start(bf16[4,32,2048]{2,1,0:T(8,128)(2,1)S(1)} %get-tuple-element.51), channel_id=1, source_target_pairs={{0,64},{8,72},{16,80},{24,88},{32,96},{40,104},{48,112},{56,120},{... | collective-permute-start | bytes 1572872 | tf_op jit(solution)/shard_map/ppermute | solution.py:27
  105.3 7.4 %collective-permute-done.30.refs_1_ = bf16[4,32,2048]{2,1,0:T(8,128)(2,1)S(1)} collective-permute-done((bf16[4,32,2048]{2,1,0:T(8,128)(2,1)S(1)}, bf16[4,32,2048]{2,1,0:T(8,128)(2,1)S(1)}, u32[]{:S(2)}, u32[]{:S(2)}) %collective-permute-start.30) | collective-permute-done | bytes 524320 | tf_op jit(solution)/shard_map/ppermute | solution.py:32
  115.3 9.8 %collective-permute-done.31.refs_2_ = bf16[4,32,2048]{2,1,0:T(8,128)(2,1)S(1)} collective-permute-done((bf16[4,32,2048]{2,1,0:T(8,128)(2,1)S(1)}, bf16[4,32,2048]{2,1,0:T(8,128)(2,1)S(1)}, u32[]{:S(2)}, u32[]{:S(2)}) %collective-permute-start.31) | collective-permute-done | bytes 524320 | tf_op jit(solution)/shard_map/ppermute | solution.py:32
  126.1 3.9 %collective-permute-start.23 = (bf16[4,32,2048]{2,1,0:T(8,128)(2,1)S(1)}, bf16[4,32,2048]{2,1,0:T(8,128)(2,1)S(1)}, u32[]{:S(2)}, u32[]{:S(2)}) collective-permute-start(bf16[4,32,2048]{2,1,0:T(8,128)(2,1)S(1)} %get-tuple-element.36), channel_id=1, source_target_pairs={{0,24},{8,0},{16,8},{24,16},{32,56},{40,32},{48,40},{56,48},{64,88... | collective-permute-start | bytes 1572872 | tf_op jit(solution)/shard_map/ppermute | solution.py:32
  130.0 3.6 %collective-permute-start.25 = (bf16[4,32,2048]{2,1,0:T(8,128)(2,1)S(1)}, bf16[4,32,2048]{2,1,0:T(8,128)(2,1)S(1)}, u32[]{:S(2)}, u32[]{:S(2)}) collective-permute-start(bf16[4,32,2048]{2,1,0:T(8,128)(2,1)S(1)} %get-tuple-element.39), channel_id=1, source_target_pairs={{0,64},{8,72},{16,80},{24,88},{32,96},{40,104},{48,112},{56,120},{... | collective-permute-start | bytes 1572872 | tf_op jit(solution)/shard_map/ppermute | solution.py:27
  134.2 4.3 %maximum_maximum_fusion.left = bf16[4,512,2048]{2,1,0:T(8,128)(2,1)S(1)} fusion(bf16[4,256,1024]{2,1,0:T(8,128)(2,1)} %bitcast.6, bf16[4,256,1024]{2,1,0:T(8,128)(2,1)} %bitcast.5, bf16[4,256,1024]{2,1,0:T(8,128)(2,1)} %bitcast.4, bf16[4,256,1024]{2,1,0:T(8,128)(2,1)} %bitcast.3), kind=kLoop, calls=%fused_computation | loop fusion | flops 33554432 | bytes 16777216 | tf_op jit(solution)/shard_map/concatenate | solution.py:276
  138.5 7.4 %shard_map.49 = (f32[48,32,128]{2,1,0:T(8,128)S(1)}, s16[1584,128]{1,0:T(8,128)(2,1)S(1)}, s16[1584,128]{1,0:T(8,128)(2,1)S(1)}, s16[1584,128]{1,0:T(8,128)(2,1)S(1)}) custom-call(s32[117]{0:T(128)S(1)} %pad_add_fusion.lists, bf16[4,512,2048]{2,1,0:T(8,128)(2,1)S(1)} %maximum_maximum_fusion.left, bf16[4,32,2048]{2,1,0:T(8,128)(2,1)S(1)} %get-tuple-element.45.refs_0_, ...), custom_call_target="tpu_custom_call" | custom-call | tf_op jit(solution)/shard_map/pallas_call | solution.py:185
  147.5 5.6 %collective-permute-done.25.refs_8_ = bf16[4,32,2048]{2,1,0:T(8,128)(2,1)S(1)} collective-permute-done((bf16[4,32,2048]{2,1,0:T(8,128)(2,1)S(1)}, bf16[4,32,2048]{2,1,0:T(8,128)(2,1)S(1)}, u32[]{:S(2)}, u32[]{:S(2)}) %collective-permute-start.25) | collective-permute-done | bytes 524320 | tf_op jit(solution)/shard_map/ppermute | solution.py:27
  154.0 7.4 %shard_map.47 = (f32[48,32,128]{2,1,0:T(8,128)S(1)}, s16[1584,128]{1,0:T(8,128)(2,1)S(1)}, s16[1584,128]{1,0:T(8,128)(2,1)S(1)}, s16[1584,128]{1,0:T(8,128)(2,1)S(1)}) custom-call(s32[117]{0:T(128)S(1)} %pad_add_fusion.lists, bf16[4,512,2048]{2,1,0:T(8,128)(2,1)S(1)} %maximum_maximum_fusion.left, bf16[4,32,2048]{2,1,0:T(8,128)(2,1)S(1)} %get-tuple-element.33.refs_0_, ...), custom_call_target="tpu_custom_call" | custom-call | tf_op jit(solution)/shard_map/pallas_call | solution.py:185
  162.7 2.6 %collective-permute-start.37 = (s16[1584,128]{1,0:T(8,128)(2,1)S(1)}, s16[1584,128]{1,0:T(8,128)(2,1)S(1)}, u32[]{:S(2)}, u32[]{:S(2)}) collective-permute-start(s16[1584,128]{1,0:T(8,128)(2,1)S(1)} %get-tuple-element.55), channel_id=1, source_target_pairs={{0,4},{1,5},{2,6},{3,7},{4,0},{5,1},{6,2},{7,3},{8,12},{9,13},{10,... | collective-permute-start | bytes 1216520 | tf_op jit(solution)/shard_map/ppermute | solution.py:37
  169.2 10.4 %collective-permute-done.37.refs_1_ = s16[1584,128]{1,0:T(8,128)(2,1)S(1)} collective-permute-done((s16[1584,128]{1,0:T(8,128)(2,1)S(1)}, s16[1584,128]{1,0:T(8,128)(2,1)S(1)}, u32[]{:S(2)}, u32[]{:S(2)}) %collective-permute-start.37) | collective-permute-done | bytes 405536 | tf_op jit(solution)/shard_map/ppermute | solution.py:37
  179.6 4.1 %collective-permute-done.38.refs_2_ = s16[1584,128]{1,0:T(8,128)(2,1)S(1)} collective-permute-done((s16[1584,128]{1,0:T(8,128)(2,1)S(1)}, s16[1584,128]{1,0:T(8,128)(2,1)S(1)}, u32[]{:S(2)}, u32[]{:S(2)}) %collective-permute-start.38) | collective-permute-done | bytes 405536 | tf_op jit(solution)/shard_map/ppermute | solution.py:37
  184.4 3.9 %collective-permute-done.28.refs_1_ = s16[1584,128]{1,0:T(8,128)(2,1)S(1)} collective-permute-done((s16[1584,128]{1,0:T(8,128)(2,1)S(1)}, s16[1584,128]{1,0:T(8,128)(2,1)S(1)}, u32[]{:S(2)}, u32[]{:S(2)}) %collective-permute-start.28) | collective-permute-done | bytes 405536 | tf_op jit(solution)/shard_map/ppermute | solution.py:37
  188.3 10.2 %collective-permute-done.29.refs_2_ = s16[1584,128]{1,0:T(8,128)(2,1)S(1)} collective-permute-done((s16[1584,128]{1,0:T(8,128)(2,1)S(1)}, s16[1584,128]{1,0:T(8,128)(2,1)S(1)}, u32[]{:S(2)}, u32[]{:S(2)}) %collective-permute-start.29) | collective-permute-done | bytes 405536 | tf_op jit(solution)/shard_map/ppermute | solution.py:37
  199.5 2.8 %collective-permute-start.39 = (f32[24,32,128]{2,1,0:T(8,128)S(1)}, f32[24,32,128]{2,1,0:T(8,128)S(1)}, u32[]{:S(2)}, u32[]{:S(2)}) collective-permute-start(f32[24,32,128]{2,1,0:T(8,128)S(1)} %get-tuple-element.60), channel_id=1, source_target_pairs={{0,1},{1,0},{2,3},{3,2},{4,5},{5,4},{6,7},{7,6},{8,9},{9,8},{10,11... | collective-permute-start | bytes 1179656 | tf_op jit(solution)/shard_map/ppermute | solution.py:41
  (103 shorter events, 55.9 us)
Async XLA Ops:
  7.5 26.8 %collective-permute-start.9 = (bf16[2,64,2048]{2,1,0:T(8,128)(2,1)S(1)}, bf16[2,64,2048]{2,1,0:T(8,128)(2,1)S(1)}, u32[]{:S(2)}, u32[]{:S(2)}) collective-permute-start(bf16[2,64,2048]{2,1,0:T(8,128)(2,1)S(1)} %pad_maximum_fusion.1.refs_0_.refs_4_), channel_id=1, source_target_pairs={{0,32},{8,40},{16,48},{24,56},{32,64},{40,72},{48,80},{56,88},{64,... | collective-permute-start | bytes 1572872 | tf_op jit(solution)/shard_map/ppermute | solution.py:27
  8.8 27.4 %collective-permute-start.10 = (bf16[2,64,2048]{2,1,0:T(8,128)(2,1)S(1)}, bf16[2,64,2048]{2,1,0:T(8,128)(2,1)S(1)}, u32[]{:S(2)}, u32[]{:S(2)}) collective-permute-start(bf16[2,64,2048]{2,1,0:T(8,128)(2,1)S(1)} %pad_maximum_fusion.2.refs_1_.refs_5_), channel_id=1, source_target_pairs={{0,32},{8,40},{16,48},{24,56},{32,64},{40,72},{48,80},{56,88},{64,... | collective-permute-start | bytes 1572872 | tf_op jit(solution)/shard_map/ppermute | solution.py:27
  10.1 28.5 %collective-permute-start.12 = (bf16[2,64,2048]{2,1,0:T(8,128)(2,1)S(1)}, bf16[2,64,2048]{2,1,0:T(8,128)(2,1)S(1)}, u32[]{:S(2)}, u32[]{:S(2)}) collective-permute-start(bf16[2,64,2048]{2,1,0:T(8,128)(2,1)S(1)} %pad_maximum_fusion.2.refs_1_.refs_5_), channel_id=1, source_target_pairs={{0,96},{8,104},{16,112},{24,120},{32,0},{40,8},{48,16},{56,24},{64... | collective-permute-start | bytes 1572872 | tf_op jit(solution)/shard_map/ppermute | solution.py:27
  15.6 18.2 %collective-permute-start.6 = (s32[16]{0:T(128)S(1)}, s32[16]{0:T(128)S(1)}, u32[]{:S(2)}, u32[]{:S(2)}) collective-permute-start(s32[16]{0:T(128)S(1)} %select_reduce_fusion.4), channel_id=1, source_target_pairs={{0,64},{8,72},{16,80},{24,88},{32,96},{40,104},{48,112},{56,120},{... | collective-permute-start | bytes 200 | tf_op jit(solution)/shard_map/ppermute | solution.py:27
  34.3 24.1 %collective-permute-start.16 = (bf16[2,64,2048]{2,1,0:T(8,128)(2,1)S(1)}, bf16[2,64,2048]{2,1,0:T(8,128)(2,1)}, u32[]{:S(2)}, u32[]{:S(2)}) collective-permute-start(bf16[2,64,2048]{2,1,0:T(8,128)(2,1)S(1)} %fusion.3.refs_9_.refs_11_), channel_id=1, source_target_pairs={{0,8},{8,16},{16,24},{24,0},{32,40},{40,48},{48,56},{56,32},{64,72... | collective-permute-start | bytes 1572872 | tf_op jit(solution)/shard_map/ppermute | solution.py:32
  36.2 64.3 %collective-permute-start.1 = (bf16[1024,1024]{1,0:T(8,128)(2,1)}, bf16[1024,1024]{1,0:T(8,128)(2,1)}, u32[]{:S(2)}, u32[]{:S(2)}) collective-permute-start(bf16[1024,1024]{1,0:T(8,128)(2,1)} %param.5), channel_id=1, source_target_pairs={{0,1},{1,0},{2,3},{3,2},{4,5},{5,4},{6,7},{7,6},{8,9},{9,8},{10,11... | collective-permute-start | bytes 6291464 | tf_op jit(solution)/shard_map/ppermute | solution.py:41
  39.4 63.3 %collective-permute-start = (bf16[1024,1024]{1,0:T(8,128)(2,1)}, bf16[1024,1024]{1,0:T(8,128)(2,1)}, u32[]{:S(2)}, u32[]{:S(2)}) collective-permute-start(bf16[1024,1024]{1,0:T(8,128)(2,1)} %param.4), channel_id=1, source_target_pairs={{0,1},{1,0},{2,3},{3,2},{4,5},{5,4},{6,7},{7,6},{8,9},{9,8},{10,11... | collective-permute-start | bytes 6291464 | tf_op jit(solution)/shard_map/ppermute | solution.py:41
  47.9 20.6 %collective-permute-start.20 = (bf16[2,64,2048]{2,1,0:T(8,128)(2,1)S(1)}, bf16[2,64,2048]{2,1,0:T(8,128)(2,1)S(1)}, u32[]{:S(2)}, u32[]{:S(2)}) collective-permute-start(bf16[2,64,2048]{2,1,0:T(8,128)(2,1)S(1)} %pad_maximum_fusion.3.refs_8_.refs_10_), channel_id=1, source_target_pairs={{0,24},{8,0},{16,8},{24,16},{32,56},{40,32},{48,40},{56,48},{64,88... | collective-permute-start | bytes 1572872 | tf_op jit(solution)/shard_map/ppermute | solution.py:32
  98.6 26.4 %collective-permute-start.31 = (bf16[4,32,2048]{2,1,0:T(8,128)(2,1)S(1)}, bf16[4,32,2048]{2,1,0:T(8,128)(2,1)S(1)}, u32[]{:S(2)}, u32[]{:S(2)}) collective-permute-start(bf16[4,32,2048]{2,1,0:T(8,128)(2,1)S(1)} %get-tuple-element.47), channel_id=1, source_target_pairs={{0,16},{8,24},{16,0},{24,8},{32,48},{40,56},{48,32},{56,40},{64,80... | collective-permute-start | bytes 1572872 | tf_op jit(solution)/shard_map/ppermute | solution.py:32
  100.6 25.5 %collective-permute-start.32 = (bf16[4,32,2048]{2,1,0:T(8,128)(2,1)S(1)}, bf16[4,32,2048]{2,1,0:T(8,128)(2,1)S(1)}, u32[]{:S(2)}, u32[]{:S(2)}) collective-permute-start(bf16[4,32,2048]{2,1,0:T(8,128)(2,1)S(1)} %get-tuple-element.48), channel_id=1, source_target_pairs={{0,24},{8,0},{16,8},{24,16},{32,56},{40,32},{48,40},{56,48},{64,88... | collective-permute-start | bytes 1572872 | tf_op jit(solution)/shard_map/ppermute | solution.py:32
  102.6 27.4 %collective-permute-start.33 = (bf16[4,32,2048]{2,1,0:T(8,128)(2,1)S(1)}, bf16[4,32,2048]{2,1,0:T(8,128)(2,1)S(1)}, u32[]{:S(2)}, u32[]{:S(2)}) collective-permute-start(bf16[4,32,2048]{2,1,0:T(8,128)(2,1)S(1)} %get-tuple-element.50), channel_id=1, source_target_pairs={{0,32},{8,40},{16,48},{24,56},{32,64},{40,72},{48,80},{56,88},{64,... | collective-permute-start | bytes 1572872 | tf_op jit(solution)/shard_map/ppermute | solution.py:27
  102.6 27.3 %collective-permute-start.34 = (bf16[4,32,2048]{2,1,0:T(8,128)(2,1)S(1)}, bf16[4,32,2048]{2,1,0:T(8,128)(2,1)S(1)}, u32[]{:S(2)}, u32[]{:S(2)}) collective-permute-start(bf16[4,32,2048]{2,1,0:T(8,128)(2,1)S(1)} %get-tuple-element.51), channel_id=1, source_target_pairs={{0,64},{8,72},{16,80},{24,88},{32,96},{40,104},{48,112},{56,120},{... | collective-permute-start | bytes 1572872 | tf_op jit(solution)/shard_map/ppermute | solution.py:27
  112.7 20.8 %collective-permute-start.35 = (bf16[4,32,2048]{2,1,0:T(8,128)(2,1)S(1)}, bf16[4,32,2048]{2,1,0:T(8,128)(2,1)S(1)}, u32[]{:S(2)}, u32[]{:S(2)}) collective-permute-start(bf16[4,32,2048]{2,1,0:T(8,128)(2,1)S(1)} %get-tuple-element.52), channel_id=1, source_target_pairs={{0,96},{8,104},{16,112},{24,120},{32,0},{40,8},{48,16},{56,24},{64... | collective-permute-start | bytes 1572872 | tf_op jit(solution)/shard_map/ppermute | solution.py:27
  125.0 20.9 %collective-permute-start.22 = (bf16[4,32,2048]{2,1,0:T(8,128)(2,1)S(1)}, bf16[4,32,2048]{2,1,0:T(8,128)(2,1)S(1)}, u32[]{:S(2)}, u32[]{:S(2)}) collective-permute-start(bf16[4,32,2048]{2,1,0:T(8,128)(2,1)S(1)} %get-tuple-element.35), channel_id=1, source_target_pairs={{0,16},{8,24},{16,0},{24,8},{32,48},{40,56},{48,32},{56,40},{64,80... | collective-permute-start | bytes 1572872 | tf_op jit(solution)/shard_map/ppermute | solution.py:32
  126.1 21.4 %collective-permute-start.23 = (bf16[4,32,2048]{2,1,0:T(8,128)(2,1)S(1)}, bf16[4,32,2048]{2,1,0:T(8,128)(2,1)S(1)}, u32[]{:S(2)}, u32[]{:S(2)}) collective-permute-start(bf16[4,32,2048]{2,1,0:T(8,128)(2,1)S(1)} %get-tuple-element.36), channel_id=1, source_target_pairs={{0,24},{8,0},{16,8},{24,16},{32,56},{40,32},{48,40},{56,48},{64,88... | collective-permute-start | bytes 1572872 | tf_op jit(solution)/shard_map/ppermute | solution.py:32
  130.0 17.5 %collective-permute-start.24 = (bf16[4,32,2048]{2,1,0:T(8,128)(2,1)S(1)}, bf16[4,32,2048]{2,1,0:T(8,128)(2,1)S(1)}, u32[]{:S(2)}, u32[]{:S(2)}) collective-permute-start(bf16[4,32,2048]{2,1,0:T(8,128)(2,1)S(1)} %get-tuple-element.38), channel_id=1, source_target_pairs={{0,32},{8,40},{16,48},{24,56},{32,64},{40,72},{48,80},{56,88},{64,... | collective-permute-start | bytes 1572872 | tf_op jit(solution)/shard_map/ppermute | solution.py:27
  130.0 23.1 %collective-permute-start.25 = (bf16[4,32,2048]{2,1,0:T(8,128)(2,1)S(1)}, bf16[4,32,2048]{2,1,0:T(8,128)(2,1)S(1)}, u32[]{:S(2)}, u32[]{:S(2)}) collective-permute-start(bf16[4,32,2048]{2,1,0:T(8,128)(2,1)S(1)} %get-tuple-element.39), channel_id=1, source_target_pairs={{0,64},{8,72},{16,80},{24,88},{32,96},{40,104},{48,112},{56,120},{... | collective-permute-start | bytes 1572872 | tf_op jit(solution)/shard_map/ppermute | solution.py:27
  133.6 20.4 %collective-permute-start.26 = (bf16[4,32,2048]{2,1,0:T(8,128)(2,1)S(1)}, bf16[4,32,2048]{2,1,0:T(8,128)(2,1)S(1)}, u32[]{:S(2)}, u32[]{:S(2)}) collective-permute-start(bf16[4,32,2048]{2,1,0:T(8,128)(2,1)S(1)} %get-tuple-element.40), channel_id=1, source_target_pairs={{0,96},{8,104},{16,112},{24,120},{32,0},{40,8},{48,16},{56,24},{64... | collective-permute-start | bytes 1572872 | tf_op jit(solution)/shard_map/ppermute | solution.py:27
  145.9 20.7 %collective-permute-start.36 = (s16[1584,128]{1,0:T(8,128)(2,1)S(1)}, s16[1584,128]{1,0:T(8,128)(2,1)S(1)}, u32[]{:S(2)}, u32[]{:S(2)}) collective-permute-start(s16[1584,128]{1,0:T(8,128)(2,1)S(1)} %get-tuple-element.54), channel_id=1, source_target_pairs={{0,2},{1,3},{2,4},{3,5},{4,6},{5,7},{6,0},{7,1},{8,10},{9,11},{10,... | collective-permute-start | bytes 1216520 | tf_op jit(solution)/shard_map/ppermute | solution.py:37
  161.3 23.0 %collective-permute-start.27 = (s16[1584,128]{1,0:T(8,128)(2,1)S(1)}, s16[1584,128]{1,0:T(8,128)(2,1)S(1)}, u32[]{:S(2)}, u32[]{:S(2)}) collective-permute-start(s16[1584,128]{1,0:T(8,128)(2,1)S(1)} %get-tuple-element.42), channel_id=1, source_target_pairs={{0,2},{1,3},{2,4},{3,5},{4,6},{5,7},{6,0},{7,1},{8,10},{9,11},{10,... | collective-permute-start | bytes 1216520 | tf_op jit(solution)/shard_map/ppermute | solution.py:37
  162.7 16.9 %collective-permute-start.37 = (s16[1584,128]{1,0:T(8,128)(2,1)S(1)}, s16[1584,128]{1,0:T(8,128)(2,1)S(1)}, u32[]{:S(2)}, u32[]{:S(2)}) collective-permute-start(s16[1584,128]{1,0:T(8,128)(2,1)S(1)} %get-tuple-element.55), channel_id=1, source_target_pairs={{0,4},{1,5},{2,6},{3,7},{4,0},{5,1},{6,2},{7,3},{8,12},{9,13},{10,... | collective-permute-start | bytes 1216520 | tf_op jit(solution)/shard_map/ppermute | solution.py:37
  165.3 18.4 %collective-permute-start.38 = (s16[1584,128]{1,0:T(8,128)(2,1)S(1)}, s16[1584,128]{1,0:T(8,128)(2,1)S(1)}, u32[]{:S(2)}, u32[]{:S(2)}) collective-permute-start(s16[1584,128]{1,0:T(8,128)(2,1)S(1)} %get-tuple-element.56), channel_id=1, source_target_pairs={{0,6},{1,7},{2,0},{3,1},{4,2},{5,3},{6,4},{7,5},{8,14},{9,15},{10,... | collective-permute-start | bytes 1216520 | tf_op jit(solution)/shard_map/ppermute | solution.py:37
  166.4 21.9 %collective-permute-start.28 = (s16[1584,128]{1,0:T(8,128)(2,1)S(1)}, s16[1584,128]{1,0:T(8,128)(2,1)S(1)}, u32[]{:S(2)}, u32[]{:S(2)}) collective-permute-start(s16[1584,128]{1,0:T(8,128)(2,1)S(1)} %get-tuple-element.43), channel_id=1, source_target_pairs={{0,4},{1,5},{2,6},{3,7},{4,0},{5,1},{6,2},{7,3},{8,12},{9,13},{10,... | collective-permute-start | bytes 1216520 | tf_op jit(solution)/shard_map/ppermute | solution.py:37
  166.6 31.9 %collective-permute-start.29 = (s16[1584,128]{1,0:T(8,128)(2,1)S(1)}, s16[1584,128]{1,0:T(8,128)(2,1)S(1)}, u32[]{:S(2)}, u32[]{:S(2)}) collective-permute-start(s16[1584,128]{1,0:T(8,128)(2,1)S(1)} %get-tuple-element.44), channel_id=1, source_target_pairs={{0,6},{1,7},{2,0},{3,1},{4,2},{5,3},{6,4},{7,5},{8,14},{9,15},{10,... | collective-permute-start | bytes 1216520 | tf_op jit(solution)/shard_map/ppermute | solution.py:37
  (23 other events, 174.4 us)
